TPU v7x, 32 devices: a whole 2x2x4 slice. The times are simulated.
32 devices in a mesh: seq: 8 (over y, x, core), mp: 4 (over z).
Axes of the slice: x: 2, y: 2, z: 4, core: 2. Of those that a mesh axis runs over, the one named last changes fastest.
Arguments:
- tokens: bfloat16 [16384, 768], P('seq'), may hold values from -6 to 6
- cotangent: bfloat16 [16384, 768], P('seq'), may hold values from -6 to 6
- past_state: bfloat16 [16, 512, 768], P('seq', None, 'mp'), may hold values from -6 to 6
- positions: int32 [16, 128], P('seq'), may hold values from 0 to 511, as said below
- counts: int32 [16], P('seq'), may hold values from 16 to 128, as said below
- ln1_gain: bfloat16 [768], P('seq'), may hold values from 0.5 to 1.5
- ln1_bias: bfloat16 [768], P('seq'), may hold values from -1 to 1
- w_qkv: bfloat16 [3, 768, 768], P(None, 'seq', 'mp'), may hold values from -0.21875 to 0.21875
- b_qv: bfloat16 [2, 12, 64], P(None, 'mp', 'seq'), may hold values from -1.5 to 1.5
- w_out: bfloat16 [768, 768], P('mp', 'seq'), may hold values from -3 to 3
- b_out: bfloat16 [768], P('seq'), may hold values from -1.5 to 1.5
- ln2_gain: bfloat16 [768], P('seq'), may hold values from 0.5 to 1.5
- ln2_bias: bfloat16 [768], P('seq'), may hold values from -1 to 1
- w_up: bfloat16 [768, 3072], P('seq', 'mp'), may hold values from -0.25 to 0.25
- b_up: bfloat16 [48, 64], P('mp', 'seq'), may hold values from -2.5 to 2.5
- w_down: bfloat16 [3072, 768], P('mp', 'seq'), may hold values from -0.109375 to 0.109375
- b_down: bfloat16 [768], P('seq'), may hold values from -1.5 to 1.5
Outputs:
- out: bfloat16 [16384, 768], P('seq')
- tokens_grad: bfloat16 [16384, 768], P('seq')
- past_grad: float32 [16, 512, 768], P('seq', None, 'mp')
- ln1_gain_grad: float32 [768], P('seq')
- ln1_bias_grad: float32 [768], P('seq')
- w_qkv_grad: float32 [3, 768, 768], P(None, 'seq', 'mp')
- b_qv_grad: float32 [2, 12, 64], P(None, 'mp', 'seq')
- w_out_grad: float32 [768, 768], P('mp', 'seq')
- b_out_grad: float32 [768], P('seq')
- ln2_gain_grad: float32 [768], P('seq')
- ln2_bias_grad: float32 [768], P('seq')
- w_up_grad: float32 [768, 3072], P('seq', 'mp')
- b_up_grad: float32 [48, 64], P('mp', 'seq')
- w_down_grad: float32 [3072, 768], P('mp', 'seq')
- b_down_grad: float32 [768], P('seq')
Inputs may be any that keep to these rules, and one draw needn't show every extreme that they name: The 128 positions of one old segment are distinct. Slots 0 to counts[i] - 1 of old segment i are used; some old segment uses all 128.
All inputs are finite; a program needn't handle non-finite values.
Results may differ from a plain program's by a relative error of at most 0.03.
Values may be sent and summed in bfloat16 or wider, within the bound.
A program may use at most 192 MiB of HBM per device.

v0:
```python
import math

import jax
import jax.numpy as jnp
from jax import lax
from jax.sharding import PartitionSpec as P

NB = 256
SEG = 512
MICRO = 2


NORM_EPSILON = 1e-05
RIDGE_WEIGHT = 1.0
NARROW_WIDTH = 0.01
BROAD_WIDTH = 0.05
GELU_SCALE = 0.7978845608028654
GELU_CUBIC = 0.044715


def as_sent(shard):
    return jax.tree.map(lambda a: a.astype(jnp.bfloat16) if a.dtype == jnp.float32 else a, shard)


def norm_rows(values, gain, bias):
    centered = values - jnp.mean(values, axis=-1, keepdims=True)
    inverse = lax.rsqrt(jnp.mean(centered * centered, axis=-1, keepdims=True) + NORM_EPSILON)
    normed = centered * inverse
    return (normed * gain + bias, normed, inverse)


def norm_back(upstream, normed, inverse, gain):
    scaled = upstream * gain
    inner = scaled - jnp.mean(scaled, axis=-1, keepdims=True)
    inner = inner - normed * jnp.mean(scaled * normed, axis=-1, keepdims=True)
    return inner * inverse


def norm_stats(upstream, normed):
    return (jnp.sum(upstream * normed, axis=0), jnp.sum(upstream, axis=0))


def gelu_tanh(inputs):
    return (
        0.5
        * inputs
        * (1.0 + jnp.tanh(GELU_SCALE * (inputs + GELU_CUBIC * inputs * inputs * inputs)))
    )


def score_blocks(queries, key_rows, memory_keys, scaling):
    window = (
        jnp.einsum("glhe,gmhe->ghlm", queries, key_rows, preferred_element_type=jnp.float32)
        * scaling
    )
    recall = (
        jnp.einsum("glhe,nhe->ghln", queries, memory_keys, preferred_element_type=jnp.float32)
        * scaling
    )
    length = queries.shape[1]
    causal = jnp.arange(length)[:, None] >= jnp.arange(length)[None, :]
    return (jnp.where(causal, window, -1e30), recall)


def attend(queries, key_rows, values, memory_keys, memory_values, scaling):
    window, recall = score_blocks(queries, key_rows, memory_keys, scaling)
    largest = jnp.maximum(
        jnp.max(window, axis=-1, keepdims=True), jnp.max(recall, axis=-1, keepdims=True)
    )
    total = jnp.sum(jnp.exp(window - largest), axis=-1, keepdims=True)
    total = total + jnp.sum(jnp.exp(recall - largest), axis=-1, keepdims=True)
    log_total = largest + jnp.log(total)
    window_probs = jnp.exp(window - log_total).astype(jnp.bfloat16)
    recall_probs = jnp.exp(recall - log_total).astype(jnp.bfloat16)
    output = jnp.einsum("ghlm,gmhe->glhe", window_probs, values, preferred_element_type=jnp.float32)
    output = output + jnp.einsum(
        "ghln,nhe->glhe", recall_probs, memory_values, preferred_element_type=jnp.float32
    )
    return (output, log_total)


def attend_back(
    queries, key_rows, values, memory_keys, memory_values, log_total, out_grad, scaling
):
    window, recall = score_blocks(queries, key_rows, memory_keys, scaling)
    window_probs = jnp.exp(window - log_total)
    recall_probs = jnp.exp(recall - log_total)
    value_grad = jnp.einsum(
        "ghlm,glhe->gmhe",
        window_probs.astype(jnp.bfloat16),
        out_grad,
        preferred_element_type=jnp.float32,
    )
    memory_value_grad = jnp.einsum(
        "ghln,glhe->nhe",
        recall_probs.astype(jnp.bfloat16),
        out_grad,
        preferred_element_type=jnp.float32,
    )
    window_dprob = jnp.einsum(
        "glhe,gmhe->ghlm", out_grad, values, preferred_element_type=jnp.float32
    )
    recall_dprob = jnp.einsum(
        "glhe,nhe->ghln", out_grad, memory_values, preferred_element_type=jnp.float32
    )
    inner = jnp.sum(window_probs * window_dprob, axis=-1, keepdims=True)
    inner = inner + jnp.sum(recall_probs * recall_dprob, axis=-1, keepdims=True)
    window_score_grad = (window_probs * (window_dprob - inner)).astype(jnp.bfloat16)
    recall_score_grad = (recall_probs * (recall_dprob - inner)).astype(jnp.bfloat16)
    query_grad = jnp.einsum(
        "ghlm,gmhe->glhe", window_score_grad, key_rows, preferred_element_type=jnp.float32
    )
    query_grad = (
        query_grad
        + jnp.einsum(
            "ghln,nhe->glhe", recall_score_grad, memory_keys, preferred_element_type=jnp.float32
        )
    ) * scaling
    key_grad = (
        jnp.einsum(
            "ghlm,glhe->gmhe", window_score_grad, queries, preferred_element_type=jnp.float32
        )
        * scaling
    )
    memory_key_grad = (
        jnp.einsum("ghln,glhe->nhe", recall_score_grad, queries, preferred_element_type=jnp.float32)
        * scaling
    )
    return (query_grad, key_grad, value_grad, memory_key_grad, memory_value_grad)


def local(
    tokens,
    cotangent,
    past_state,
    positions,
    counts,
    ln1_gain,
    ln1_bias,
    w_qkv,
    b_qv,
    w_out,
    b_out,
    ln2_gain,
    ln2_bias,
    w_up,
    b_up,
    w_down,
    b_down,
):
    highest = lax.Precision.HIGHEST
    shards = (
        w_qkv,
        w_out,
        w_up,
        w_down,
        b_qv,
        b_up,
        b_out,
        b_down,
        ln1_gain,
        ln1_bias,
        ln2_gain,
        ln2_bias,
    )
    item_count, seg_len, local_width = past_state.shape
    slots = positions.shape[1]
    seq_index = lax.axis_index("seq")
    total_items = item_count * lax.axis_size("seq")
    item_ids = (seq_index * item_count + jnp.arange(item_count)).astype(jnp.float32)
    places = (item_ids[:, None] + (positions.astype(jnp.float32) + 0.5) / seg_len) / total_items
    centers = (jnp.arange(NB, dtype=jnp.float32) + 0.5) / NB
    widths = jnp.where(jnp.arange(NB) % 2 == 0, NARROW_WIDTH, BROAD_WIDTH).astype(jnp.float32)
    slot_used = (jnp.arange(slots)[None, :] < counts[:, None]).astype(jnp.float32)
    basis_rows = (
        jnp.exp(-0.5 * jnp.square((places[:, :, None] - centers) / widths)) * slot_used[:, :, None]
    )
    basis_rows = basis_rows.reshape(item_count * slots, NB)
    sampled = jnp.take_along_axis(past_state, positions[:, :, None], axis=1)
    sampled = sampled.reshape(item_count * slots, local_width).astype(jnp.float32)
    part_moments = jnp.dot(basis_rows.T, sampled, precision=highest)
    part_gram = jnp.dot(basis_rows.T, basis_rows, precision=highest)
    identity_mat = jnp.eye(NB, dtype=jnp.float32)
    gram_mat, moments = lax.psum((part_gram, part_moments), "seq")
    factor = jnp.linalg.cholesky(gram_mat + RIDGE_WEIGHT * identity_mat)
    coef_part = jax.scipy.linalg.cho_solve((factor, True), moments)
    coefficients = lax.all_gather(as_sent(coef_part), "mp", axis=1, tiled=True).astype(
        coef_part.dtype
    )
    tok_count = tokens.shape[0] // MICRO
    mp_index = lax.axis_index("mp")
    quarter = tok_count // lax.axis_size("mp")
    row_start = mp_index * quarter
    mem_key_grad = jnp.zeros((NB, local_width), jnp.float32)
    mem_value_grad = jnp.zeros((NB, local_width), jnp.float32)
    norm_grads = None
    gradients = None
    out_rows = []
    input_grads = []
    for micro_step in range(MICRO):
        params = (
            lax.all_gather(shards[0], "seq", axis=1, tiled=True),
            lax.all_gather(shards[1], "seq", axis=1, tiled=True),
            lax.all_gather(shards[2], "seq", axis=0, tiled=True),
            lax.all_gather(shards[3], "seq", axis=1, tiled=True),
            lax.all_gather(shards[4], "seq", axis=2, tiled=True),
            lax.all_gather(shards[5], "seq", axis=1, tiled=True),
            lax.all_gather(shards[6], "seq", axis=0, tiled=True),
            lax.all_gather(shards[7], "seq", axis=0, tiled=True),
            lax.all_gather(shards[8], "seq", axis=0, tiled=True),
            lax.all_gather(shards[9], "seq", axis=0, tiled=True),
            lax.all_gather(shards[10], "seq", axis=0, tiled=True),
            lax.all_gather(shards[11], "seq", axis=0, tiled=True),
        )
        (
            wide_qkv,
            wide_out,
            wide_up,
            wide_down,
            bias_qv,
            bias_up_rows,
            bias_out,
            bias_down,
            gain_one,
            bias_one,
            gain_two,
            bias_two,
        ) = params
        head_local = bias_qv.shape[1]
        head_size = bias_qv.shape[2]
        scaling = 1.0 / math.sqrt(head_size)
        bias_query = bias_qv[0].reshape(-1)
        bias_value = bias_qv[1].reshape(-1)
        bias_up = bias_up_rows.reshape(-1)
        if micro_step == 0:
            memory_out, memory_normed, memory_inverse = norm_rows(coefficients, gain_one, bias_one)
            memory_low = memory_out.astype(jnp.bfloat16)
            memory_keys = jnp.dot(memory_low, wide_qkv[1], preferred_element_type=jnp.float32)
            memory_keys = memory_keys.astype(jnp.bfloat16).reshape(NB, head_local, head_size)
            memory_values = (
                jnp.dot(memory_low, wide_qkv[2], preferred_element_type=jnp.float32) + bias_value
            )
            memory_values = memory_values.astype(jnp.bfloat16).reshape(NB, head_local, head_size)
        start = micro_step * tok_count
        token_block = tokens[start : start + tok_count].astype(jnp.float32)
        hidden_one, normed_one, inverse_one = norm_rows(token_block, gain_one, bias_one)
        hidden_one = hidden_one.astype(jnp.bfloat16)
        queries = (
            jnp.dot(hidden_one, wide_qkv[0], preferred_element_type=jnp.float32) + bias_query
        ).astype(jnp.bfloat16)
        key_rows = jnp.dot(hidden_one, wide_qkv[1], preferred_element_type=jnp.float32).astype(
            jnp.bfloat16
        )
        values = (
            jnp.dot(hidden_one, wide_qkv[2], preferred_element_type=jnp.float32) + bias_value
        ).astype(jnp.bfloat16)
        head_shape = (tok_count // SEG, SEG, head_local, head_size)
        queries = queries.reshape(head_shape)
        key_rows = key_rows.reshape(head_shape)
        values = values.reshape(head_shape)
        attended, log_total = attend(queries, key_rows, values, memory_keys, memory_values, scaling)
        attended = attended.reshape(tok_count, local_width).astype(jnp.bfloat16)
        attn_part = jnp.dot(attended, wide_out, preferred_element_type=jnp.float32)
        residual = (
            token_block
            + lax.psum(attn_part.astype(jnp.bfloat16), "mp").astype(jnp.float32)
            + bias_out
        )
        hidden_two, normed_two, inverse_two = norm_rows(residual, gain_two, bias_two)
        hidden_two = hidden_two.astype(jnp.bfloat16)
        pre_act = jnp.dot(hidden_two, wide_up, preferred_element_type=jnp.float32) + bias_up
        activation = gelu_tanh(pre_act).astype(jnp.bfloat16)
        mlp_part = jnp.dot(activation, wide_down, preferred_element_type=jnp.float32)
        mlp_sum = lax.psum(mlp_part.astype(jnp.bfloat16), "mp").astype(jnp.float32)
        out_rows.append((residual + mlp_sum + bias_down).astype(jnp.bfloat16))
        upstream = cotangent[start : start + tok_count].astype(jnp.float32)
        mlp_grad = upstream.astype(jnp.bfloat16)
        act_grad = jnp.dot(mlp_grad, wide_down.T, preferred_element_type=jnp.float32)
        gelu_pull = jax.vjp(gelu_tanh, pre_act)[1]
        pre_grad = gelu_pull(act_grad)[0].astype(jnp.bfloat16)
        hidden_two_part = jnp.dot(pre_grad, wide_up.T, preferred_element_type=jnp.float32)
        hidden_two_grad = lax.psum(hidden_two_part.astype(jnp.bfloat16), "mp").astype(jnp.float32)
        residual_grad = upstream + norm_back(hidden_two_grad, normed_two, inverse_two, gain_two)
        stats_two = norm_stats(
            lax.dynamic_slice_in_dim(hidden_two_grad, row_start, quarter, 0),
            lax.dynamic_slice_in_dim(normed_two, row_start, quarter, 0),
        )
        attn_grad = residual_grad.astype(jnp.bfloat16)
        attended_grad = jnp.dot(attn_grad, wide_out.T, preferred_element_type=jnp.float32)
        attended_grad = attended_grad.astype(jnp.bfloat16).reshape(head_shape)
        query_grad, key_grad, value_grad, block_key_grad, block_value_grad = attend_back(
            queries, key_rows, values, memory_keys, memory_values, log_total, attended_grad, scaling
        )
        query_grad = query_grad.reshape(tok_count, local_width).astype(jnp.bfloat16)
        key_grad = key_grad.reshape(tok_count, local_width).astype(jnp.bfloat16)
        value_grad = value_grad.reshape(tok_count, local_width).astype(jnp.bfloat16)
        mem_key_grad = mem_key_grad + block_key_grad.reshape(NB, local_width)
        mem_value_grad = mem_value_grad + block_value_grad.reshape(NB, local_width)
        hidden_one_part = jnp.dot(query_grad, wide_qkv[0].T, preferred_element_type=jnp.float32)
        hidden_one_part = hidden_one_part + jnp.dot(
            key_grad, wide_qkv[1].T, preferred_element_type=jnp.float32
        )
        hidden_one_part = hidden_one_part + jnp.dot(
            value_grad, wide_qkv[2].T, preferred_element_type=jnp.float32
        )
        hidden_one_grad = lax.psum(hidden_one_part.astype(jnp.bfloat16), "mp").astype(jnp.float32)
        token_part = norm_back(hidden_one_grad, normed_one, inverse_one, gain_one)
        stats_one = norm_stats(
            lax.dynamic_slice_in_dim(hidden_one_grad, row_start, quarter, 0),
            lax.dynamic_slice_in_dim(normed_one, row_start, quarter, 0),
        )
        input_grads.append((residual_grad + token_part).astype(jnp.bfloat16))
        micro_norms = jnp.stack([stats_one[0], stats_one[1], stats_two[0], stats_two[1]])
        norm_grads = micro_norms if norm_grads is None else norm_grads + micro_norms
        micro_grads = (
            jnp.stack(
                [
                    jnp.dot(hidden_one.T, query_grad, preferred_element_type=jnp.float32),
                    jnp.dot(hidden_one.T, key_grad, preferred_element_type=jnp.float32),
                    jnp.dot(hidden_one.T, value_grad, preferred_element_type=jnp.float32),
                ]
            ),
            jnp.dot(attended.T, attn_grad, preferred_element_type=jnp.float32),
            jnp.dot(hidden_two.T, pre_grad, preferred_element_type=jnp.float32),
            jnp.dot(activation.T, mlp_grad, preferred_element_type=jnp.float32),
            jnp.stack(
                [
                    jnp.sum(query_grad.astype(jnp.float32), axis=0),
                    jnp.sum(value_grad.astype(jnp.float32), axis=0),
                ]
            ).reshape(bias_qv.shape),
            jnp.sum(pre_grad.astype(jnp.float32), axis=0).reshape(bias_up_rows.shape),
            jnp.sum(attn_grad.astype(jnp.float32), axis=0),
            jnp.sum(mlp_grad.astype(jnp.float32), axis=0),
        )
        gradients = (
            micro_grads if gradients is None else jax.tree.map(jnp.add, gradients, micro_grads)
        )
    block_out = jnp.concatenate(out_rows, axis=0)
    block_input_grad = jnp.concatenate(input_grads, axis=0)
    memory_wide = memory_low.astype(jnp.float32)
    zero_block = jnp.zeros((memory_wide.shape[1], local_width), jnp.float32)
    qkv_grad = gradients[0] + jnp.stack(
        [
            zero_block,
            jnp.dot(memory_wide.T, mem_key_grad, precision=highest),
            jnp.dot(memory_wide.T, mem_value_grad, precision=highest),
        ]
    )
    bias_extra = jnp.stack(
        [jnp.zeros((local_width,), jnp.float32), jnp.sum(mem_value_grad, axis=0)]
    )
    qv_grad = gradients[4] + bias_extra.reshape(gradients[4].shape)
    memory_part = jnp.dot(mem_key_grad, wide_qkv[1].astype(jnp.float32).T, precision=highest)
    memory_part = memory_part + jnp.dot(
        mem_value_grad, wide_qkv[2].astype(jnp.float32).T, precision=highest
    )
    memory_grad, norm_total = lax.psum((memory_part, norm_grads), ("seq", "mp"))
    coef_grad = norm_back(memory_grad, memory_normed, memory_inverse, gain_one)
    gain_mem_grad, bias_mem_grad = norm_stats(memory_grad, memory_normed)
    coef_local = lax.dynamic_slice_in_dim(coef_grad, mp_index * local_width, local_width, 1)
    moment_grad = jax.scipy.linalg.cho_solve((factor, True), coef_local)
    sampled_grad = jnp.dot(basis_rows, moment_grad, precision=highest).reshape(
        item_count, slots, local_width
    )
    past_grad = jnp.zeros((item_count, seg_len, local_width), jnp.float32)
    past_grad = past_grad.at[jnp.arange(item_count)[:, None], positions].add(sampled_grad)
    summed = (
        lax.psum_scatter(qkv_grad, "seq", scatter_dimension=1, tiled=True),
        lax.psum_scatter(gradients[1], "seq", scatter_dimension=1, tiled=True),
        lax.psum_scatter(gradients[2], "seq", scatter_dimension=0, tiled=True),
        lax.psum_scatter(gradients[3], "seq", scatter_dimension=1, tiled=True),
        lax.psum_scatter(qv_grad, "seq", scatter_dimension=2, tiled=True),
        lax.psum_scatter(gradients[5], "seq", scatter_dimension=1, tiled=True),
        lax.psum_scatter(gradients[6], "seq", scatter_dimension=0, tiled=True),
        lax.psum_scatter(gradients[7], "seq", scatter_dimension=0, tiled=True),
    )
    shard_width = ln1_gain.shape[0]
    norm_slice = lax.dynamic_slice_in_dim(norm_total, seq_index * shard_width, shard_width, 1)
    gain_slice = lax.dynamic_slice_in_dim(gain_mem_grad, seq_index * shard_width, shard_width, 0)
    bias_slice = lax.dynamic_slice_in_dim(bias_mem_grad, seq_index * shard_width, shard_width, 0)
    return (
        block_out,
        block_input_grad,
        past_grad,
        norm_slice[0] + gain_slice,
        norm_slice[1] + bias_slice,
        summed[0],
        summed[4],
        summed[1],
        summed[6],
        norm_slice[2],
        norm_slice[3],
        summed[2],
        summed[5],
        summed[3],
        summed[7],
    )


def solution(mesh):
    placed = (
        P("seq", None),
        P("seq", None),
        P("seq", None, "mp"),
        P("seq", None),
        P("seq"),
        P("seq"),
        P("seq"),
        P(None, "seq", "mp"),
        P(None, "mp", "seq"),
        P("mp", "seq"),
        P("seq"),
        P("seq"),
        P("seq"),
        P("seq", "mp"),
        P("mp", "seq"),
        P("mp", "seq"),
        P("seq"),
    )
    return jax.shard_map(
        local,
        mesh=mesh,
        in_specs=placed,
        out_specs=(
            P("seq", None),
            P("seq", None),
            P("seq", None, "mp"),
            P("seq"),
            P("seq"),
            P(None, "seq", "mp"),
            P(None, "mp", "seq"),
            P("mp", "seq"),
            P("seq"),
            P("seq"),
            P("seq"),
            P("seq", "mp"),
            P("mp", "seq"),
            P("mp", "seq"),
            P("seq"),
        ),
        check_vma=False,
    )
```

profile of v0, /device:TPU:0, one launch (start us, length us, event | category | flops | bytes accessed | tf_op | source)
XLA Modules:
  0.0 1186.5 jit_solution(807040531072143628)
XLA Ops:
  12.3 2.8 gather_fusion
  20.6 25.6 %all-reduce.14 = (bf16[768]{0:T(1024)(128)(2,1)S(1)}, bf16[768]{0:T(1024)(128)(2,1)S(1)}, bf16[768]{0:T(1024)(128)(2,1)}, bf16[768]{0:T(1024)(128)(2,1)}, bf16[768]{0:T(1024)(128)(2,1)}, /*index=5*/bf16[768]{0:T(1024)(128)(2,1)}) all-reduce(bf16[768]{0:T(1024)(128)(2,1)S(1)} %dynamic-update-slice.13, ...), channel_id=1, replica_groups=mesh['seq'=8,'mp'=4] {'seq'}, use_global_device_ids=true, to_apply=%add.3 | all-reduce | flops 4608 | bytes 18432
  48.1 8.6 all_gather.54
  57.2 12.3 %all_gather.53 = bf16[3,768,192]{2,1,0:T(8,128)(2,1)S(1)} all-gather(bf16[3,96,192]{2,1,0:T(8,128)(2,1)} %param.26), channel_id=1, replica_groups=mesh['seq'=8,'mp'=4] {'seq'}, dimensions={1}, use_global_device_ids=true | all-gather | bytes 995328 | tf_op jit(solution)/shard_map/all_gather | solution.py:202
  69.5 2.3 fusion.2
  76.5 2.9 fusion.94
  79.4 2.1 reshape.400
  81.4 5.8 fusion
  91.4 10.6 all_gather.56
  107.0 11.7 cholesky.50
  119.4 10.4 custom-call.16
  132.1 11.7 cholesky.105
  147.5 5.6 while.4
  153.1 20.5 %custom-call.22 = f32[2,128,128]{1,2,0:T(8,128)S(1)} custom-call(f32[2,128,128]{2,1,0:T(8,128)} %get-tuple-element.30), custom_call_target="InvertDiagBlocksLowerTriangular" | custom-call | tf_op jit(solution)/shard_map/jit(_cho_solve)/triangular_solve | solution.py:186
  177.2 15.3 %all_gather.55 = bf16[256,768]{0,1:T(8,128)(2,1)S(1)} all-gather(bf16[256,192]{0,1:T(8,128)(2,1)S(1)} %maximum_convert_fusion), channel_id=1, replica_groups=mesh['seq'=8,'mp'=4] {'mp'}, dimensions={1}, use_global_device_ids=true | all-gather | bytes 491520 | tf_op jit(solution)/shard_map/all_gather | solution.py:187
  194.7 5.6 exponential_reduce_fusion.1
  209.7 67.3 %all-reduce.24.cloned.1.call-done = bf16[1024,768]{1,0:T(8,128)(2,1)} async-done(((bf16[1024,768]{1,0:T(8,128)(2,1)}), bf16[1024,768]{1,0:T(8,128)(2,1)}) %all-reduce.24.cloned.1.call-update) | async-done | bytes 1572880 | tf_op jit(solution)/shard_map/psum | solution.py:266
  276.9 3.1 fusion.39
  280.1 2.3 fusion.4
  307.8 10.9 all_gather.61
  322.8 49.6 %all-reduce.26.cloned.1.call-done = bf16[1024,768]{1,0:T(8,128)(2,1)} async-done(((bf16[1024,768]{1,0:T(8,128)(2,1)}), bf16[1024,768]{1,0:T(8,128)(2,1)}) %all-reduce.26.cloned.1.call-update) | async-done | bytes 1572880 | tf_op jit(solution)/shard_map/psum | solution.py:266
  372.4 3.4 multiply_reduce_fusion.7
  377.3 3.4 subtract_multiply_fusion.1
  380.7 16.6 %all-gather.3.cloned.1.call-done = bf16[768,768]{1,0:T(8,128)(2,1)} async-done(((bf16[96,768]{1,0:T(8,128)(2,1)}), bf16[768,768]{1,0:T(8,128)(2,1)}) %all-gather.3.cloned.1.call-update) | async-done | bytes 1179664 | tf_op jit(solution)/shard_map/all_gather | solution.py:204
  397.3 5.3 fusion.120
  402.5 20.6 %all-gather.5.cloned.1.call-done = bf16[768,768]{0,1:T(8,128)(2,1)} async-done(((bf16[768,96]{0,1:T(8,128)(2,1)}), bf16[768,768]{0,1:T(8,128)(2,1)}) %all-gather.5.cloned.1.call-update) | async-done | bytes 1179664 | tf_op jit(solution)/shard_map/all_gather | solution.py:205
  423.1 6.9 convert_reduce_fusion.5
  430.0 2.6 convolution_convert_fusion.1
  434.9 4.3 convert_reduce_fusion.4
  440.3 2.6 convolution_convert_fusion
  443.7 5.5 convolution_convert_fusion.4
  449.2 115.4 %all-reduce.34.cloned.1.call-done = (bf16[1024,768]{1,0:T(8,128)(2,1)}, bf16[1024,768]{1,0:T(8,128)(2,1)}) async-done(((bf16[1024,768]{1,0:T(8,128)(2,1)}, bf16[1024,768]{1,0:T(8,128)(2,1)}), (bf16[1024,768]{1,0:T(8,128)(2,1)}, bf16[1024,768]{1,0:T(8,128)(2,1)})) %all-reduce.34.cloned.1.call-update) | async-done | bytes 3145744 | tf_op jit(solution)/shard_map/psum | solution.py:282
  564.6 5.1 multiply_reduce_fusion.11
  571.0 6.1 convert_reduce_fusion.2
  582.5 3.4 convolution_bitcast_fusion.15
  586.0 6.0 convert_reduce_fusion.11
  595.4 6.0 convert_reduce_fusion.9
  601.5 2.4 fusion.27
  604.0 2.5 fusion.24
  606.5 3.6 fusion.126
  610.2 7.3 multiply_reduce_fusion.1
  618.2 9.7 multiply_convert_fusion.1
  627.9 4.1 fusion.98
  650.7 2.9 convolution_bitcast_fusion.9
  653.6 2.8 convolution_bitcast_fusion.8
  656.4 2.2 copy.504
  658.6 3.9 fusion.97
  670.9 4.2 copy.500
  675.1 4.8 reshape.486
  680.0 5.6 convolution_convert_fusion.2
  692.5 4.4 fusion.110
  696.9 3.4 convolution_add_fusion
  703.1 4.0 fusion.119
  707.1 3.0 convolution_add_fusion.1
  726.2 25.5 %all-reduce.12 = (f32[2,3,64]{2,1,0:T(4,128)}, f32[768]{0:T(1024)}, f32[12,64]{1,0:T(8,128)}, f32[768]{0:T(1024)}) all-reduce(f32[2,3,64]{2,1,0:T(4,128)S(1)} %fusion.189, f32[768]{0:T(1024)} %add.572, f32[12,64]{1,0:T(8,128)S(1)} %add.575, f32[768]{0:T(1024)} %add.577), channel_id=3, replica_groups=mesh['seq'=8,'mp'=4] {'seq'}, use_global_device_ids=true, to_apply=%region_65.67.clone | all-reduce | flops 2688 | bytes 21504
  757.0 21.7 %all-reduce.28.cloned.1.call-done = f32[256,768]{0,1:T(8,128)} async-done(((f32[256,768]{0,1:T(8,128)}), f32[256,768]{0,1:T(8,128)}) %all-reduce.28.cloned.1.call-update) | async-done | bytes 786448 | tf_op jit(solution)/shard_map/psum | solution.py:358
  784.3 29.4 %scatter_fusion = f32[2,512,192]{2,1,0:T(8,128)} fusion(f32[2,512,192]{2,1,0:T(8,128)} %broadcast_in_dim.44, s32[256]{0:T(256)S(1)} %copy-done.30, f32[256,192]{1,0:T(8,128)S(1)} %bitcast.439), kind=kCustom, calls=%fused_computation.1 | custom fusion | flops 49152 | bytes 591872 | tf_op jit(solution)/shard_map/scatter-add | solution.py:367
  813.7 2.4 copy.464
  817.9 42.5 %reduce-scatter.15.cloned.1.call-done = f32[96,576]{1,0:T(8,128)} async-done(((f32[768,576]{1,0:T(8,128)}), f32[96,576]{1,0:T(8,128)}) %reduce-scatter.15.cloned.1.call-update) | async-done | bytes 221200
  862.3 224.5 %all-reduce.32.cloned.1.call-done = (bf16[1024,768]{1,0:T(8,128)(2,1)}, bf16[1024,768]{1,0:T(8,128)(2,1)}, bf16[1024,768]{1,0:T(8,128)(2,1)}, bf16[1024,768]{1,0:T(8,128)(2,1)}) async-done(((bf16[1024,768]{1,0:T(8,128)(2,1)}, bf16[1024,768]{1,0:T(8,128)(2,1)}, bf16[1024,768]{1,0:T(8,128)(2,1)}, bf16[1024,768]{1,0:T(8,128)(2,1)}), (bf16[1024,768]{1,0:T(8,128)(2,1)}, bf16[1024,768]{1,0:T(8,128)(2,1)}, ...) | async-done | bytes 6291472 | tf_op jit(solution)/shard_map/psum | solution.py:274
  1091.5 39.3 %psum.95 = f32[4,768]{1,0:T(4,128)S(1)} all-reduce(f32[4,768]{1,0:T(4,128)S(1)} %maximum_add_fusion.1), channel_id=1, replica_groups=mesh['seq'=8,'mp'=4] {'seq','mp'}, use_global_device_ids=true, to_apply=%region_56.58 | all-reduce | flops 3072 | bytes 24576 | tf_op jit(solution)/shard_map/psum | solution.py:358
  1132.1 6.2 multiply_reduce_fusion.4
  1138.5 2.6 add_convert_fusion.2
  1144.9 34.3 %reduce-scatter.11.cloned.1.call-done = f32[96,768]{1,0:T(8,128)} async-done(((f32[768,768]{1,0:T(8,128)}), f32[96,768]{1,0:T(8,128)}) %reduce-scatter.11.cloned.1.call-update) | async-done | bytes 294928 | tf_op jit(solution)/shard_map/reduce_scatter | solution.py:371
  (622 shorter events, 171.8 us)
Async XLA Ops:
  7.2 10.8 copy-start.153
  7.2 12.0 %copy-start.166 = (bf16[96]{0:T(256)(128)(2,1)S(1)}, bf16[96]{0:T(256)(128)(2,1)}, u32[]{:S(2)}) copy-start(bf16[96]{0:T(256)(128)(2,1)} %param.30) | copy-start | bytes 580
  7.2 12.3 %copy-start.167 = (bf16[96]{0:T(256)(128)(2,1)S(1)}, bf16[96]{0:T(256)(128)(2,1)}, u32[]{:S(2)}) copy-start(bf16[96]{0:T(256)(128)(2,1)} %param.31) | copy-start | bytes 580
  7.2 12.5 %copy-start.168 = (bf16[96]{0:T(256)(128)(2,1)S(1)}, bf16[96]{0:T(256)(128)(2,1)}, u32[]{:S(2)}) copy-start(bf16[96]{0:T(256)(128)(2,1)} %param.29) | copy-start | bytes 580
  7.2 12.7 %copy-start.169 = (bf16[96]{0:T(256)(128)(2,1)S(1)}, bf16[96]{0:T(256)(128)(2,1)}, u32[]{:S(2)}) copy-start(bf16[96]{0:T(256)(128)(2,1)} %param.24) | copy-start | bytes 580
  7.2 12.9 %copy-start.170 = (bf16[96]{0:T(256)(128)(2,1)S(1)}, bf16[96]{0:T(256)(128)(2,1)}, u32[]{:S(2)}) copy-start(bf16[96]{0:T(256)(128)(2,1)} %param.25) | copy-start | bytes 580
  7.2 13.2 %copy-start.171 = (bf16[96]{0:T(256)(128)(2,1)S(1)}, bf16[96]{0:T(256)(128)(2,1)}, u32[]{:S(2)}) copy-start(bf16[96]{0:T(256)(128)(2,1)} %param.35) | copy-start | bytes 580
  7.3 39.0 %copy-start.154 = (bf16[2,3,8]{2,0,1:T(2,128)(2,1)S(1)}, bf16[2,3,8]{2,0,1:T(2,128)(2,1)}, u32[]{:S(2)}) copy-start(bf16[2,3,8]{2,0,1:T(2,128)(2,1)} %param.27) | copy-start | bytes 292
  7.3 39.1 %copy-start = (bf16[2048,768]{1,0:T(8,128)(2,1)S(1)}, bf16[2048,768]{1,0:T(8,128)(2,1)}, u32[]{:S(2)}) copy-start(bf16[2048,768]{1,0:T(8,128)(2,1)} %param.19) | copy-start | bytes 9437188
  7.3 95.3 %all-reduce.30.cloned.1.call-start = ((), (), s32[]{:S(2)}) async-start(), calls=%async_computation.13 | async-start | bytes 917504 | tf_op jit(solution)/shard_map/psum | solution.py:184
  7.3 10.5 copy-start.157
  7.3 10.5 copy-start.159
  9.5 8.3 copy-start.161
  10.3 7.6 copy-start.155
  17.7 259.2 %all-reduce.24.cloned.1.call-start = ((), (), s32[]{:S(2)}) async-start(), calls=%async_computation.4 | async-start | bytes 3145728 | tf_op jit(solution)/shard_map/psum | solution.py:266
  17.9 63.5 %copy-start.43 = (pred[512,512]{0,1:T(8,128)(4,1)}, pred[512,512]{0,1:T(8,128)(4,1)S(1)}, u32[]{:S(2)}) copy-start(pred[512,512]{0,1:T(8,128)(4,1)S(1)} %iota_compare_fusion) | copy-start | bytes 786436
  46.3 147.1 %copy-start.112 = (f32[768]{0:T(1024)}, f32[768]{0:T(1024)S(1)}, u32[]{:S(2)}) copy-start(f32[768]{0:T(1024)S(1)} %convert_element_type.366) | copy-start | bytes 9220
  46.3 147.1 %copy-start.107 = (f32[768]{0:T(1024)}, f32[768]{0:T(1024)S(1)}, u32[]{:S(2)}) copy-start(f32[768]{0:T(1024)S(1)} %convert_element_type.365) | copy-start | bytes 9220
  46.7 25.2 %copy-start.115 = (f32[1024]{0:T(1024)}, f32[1024]{0:T(1024)S(1)}, u32[]{:S(2)}) copy-start(f32[1024]{0:T(1024)S(1)} %broadcast_multiply_fusion.12) | copy-start | bytes 12292
  48.1 23.7 %copy-start.119 = (f32[1024]{0:T(1024)}, f32[1024]{0:T(1024)S(1)}, u32[]{:S(2)}) copy-start(f32[1024]{0:T(1024)S(1)} %add_rsqrt_fusion.3) | copy-start | bytes 12292
  57.0 19.5 %copy-start.143 = (f32[192]{0:T(256)}, f32[192]{0:T(256)S(1)}, u32[]{:S(2)}) copy-start(f32[192]{0:T(256)S(1)} %reshape.433) | copy-start | bytes 2308
  57.2 136.2 %copy-start.145 = (f32[192]{0:T(256)}, f32[192]{0:T(256)S(1)}, u32[]{:S(2)}) copy-start(f32[192]{0:T(256)S(1)} %reshape.432) | copy-start | bytes 2308
  153.1 24.0 %copy-start.71 = (f32[256,256]{1,0:T(8,128)}, f32[256,256]{1,0:T(8,128)S(1)}, u32[]{:S(2)}) copy-start(f32[256,256]{1,0:T(8,128)S(1)} %get-tuple-element.348) | copy-start | bytes 786436
  173.7 19.1 %copy-start.18 = (bf16[3,768,192]{2,1,0:T(8,128)(2,1)S(1)}, bf16[3,768,192]{2,1,0:T(8,128)(2,1)}, u32[]{:S(2)}) copy-start(bf16[3,768,192]{2,1,0:T(8,128)(2,1)} %copy-done.17) | copy-start | bytes 2654212
  176.1 17.9 %copy-start.51 = (bf16[2,512,3,64]{1,0,3,2:T(2,128)(2,1)S(1)}, bf16[2,512,3,64]{1,0,3,2:T(2,128)(2,1)}, u32[]{:S(2)}) copy-start(bf16[2,512,3,64]{1,0,3,2:T(2,128)(2,1)} %reshape.400) | copy-start | bytes 1179652
  194.0 9.1 copy-start.92
  194.0 7.0 slice-start
  194.7 8.5 copy-start.1
  206.9 73.2 %copy-start.108 = (f32[768]{0:T(1024)S(1)}, f32[768]{0:T(1024)}, u32[]{:S(2)}) copy-start(f32[768]{0:T(1024)} %copy-done.107) | copy-start | bytes 9220
  206.9 165.5 %all-reduce.26.cloned.1.call-start = ((), (), s32[]{:S(2)}) async-start(), calls=%async_computation.7 | async-start | bytes 3145728 | tf_op jit(solution)/shard_map/psum | solution.py:266
  304.1 93.2 %all-gather.3.cloned.1.call-start = ((), (), s32[]{:S(2)}) async-start(), calls=%async_computation.5 | async-start | bytes 1327104 | tf_op jit(solution)/shard_map/all_gather | solution.py:204
  304.7 118.4 %all-gather.5.cloned.1.call-start = ((), (), s32[]{:S(2)}) async-start(), calls=%async_computation.6 | async-start | bytes 1327104 | tf_op jit(solution)/shard_map/all_gather | solution.py:205
  305.2 259.3 %all-reduce.34.cloned.1.call-start = ((), (), s32[]{:S(2)}) async-start(), calls=%async_computation.15 | async-start | bytes 6291456 | tf_op jit(solution)/shard_map/psum | solution.py:282
  423.1 6.9 copy-start.165
  443.0 335.8 %all-reduce.28.cloned.1.call-start = ((), (), s32[]{:S(2)}) async-start(), calls=%async_computation.8 | async-start | bytes 1572864 | tf_op jit(solution)/shard_map/psum | solution.py:358
  564.6 6.5 copy-start.33
  564.6 6.5 copy-start.125
  564.6 6.5 copy-start.128
  564.6 6.5 copy-start.130
  595.4 8.5 copy-start.48
  595.4 8.5 copy-start.101
  595.4 14.7 %slice-start.4 = ((s8[6291456]{0:T(1024)(128)(4,1)}), s8[4194304]{0:T(1024)(128)(4,1)S(1)}, s32[]{:S(2)}) async-start(s8[6291456]{0:T(1024)(128)(4,1)} %bitcast.397), calls=%async_computation.20 | async-start | bytes 8388608
  601.5 8.6 slice-start.2
  601.5 8.6 slice-start.5
  618.2 9.7 copy-start.52
  627.9 14.3 %copy-start.26 = (bf16[2,3,512,512]{2,3,1,0:T(8,128)(2,1)}, bf16[2,3,512,512]{2,3,1,0:T(8,128)(2,1)S(1)}, u32[]{:S(2)}) copy-start(bf16[2,3,512,512]{2,3,1,0:T(8,128)(2,1)S(1)} %get-tuple-element.210) | copy-start | bytes 9437188
  635.8 13.3 %copy-start.80 = (f32[3,64,256]{2,1,0:T(8,128)}, f32[3,64,256]{2,1,0:T(8,128)S(1)}, u32[]{:S(2)}) copy-start(f32[3,64,256]{2,1,0:T(8,128)S(1)} %get-tuple-element.241) | copy-start | bytes 589828
  650.5 165.8 %reduce-scatter.17.cloned.1.call-start = ((), (), s32[]{:S(2)}) async-start(), calls=%async_computation.12 | async-start | bytes 884736
  662.5 197.8 %reduce-scatter.15.cloned.1.call-start = ((), (), s32[]{:S(2)}) async-start(), calls=%async_computation.11 | async-start | bytes 2211840
  679.9 406.9 %all-reduce.32.cloned.1.call-start = ((), (), s32[]{:S(2)}) async-start(), calls=%async_computation.14 | async-start | bytes 12582912 | tf_op jit(solution)/shard_map/psum | solution.py:274
  692.2 452.7 %reduce-scatter.13.cloned.1.call-start = ((), (), s32[]{:S(2)}) async-start(), calls=%async_computation.10 | async-start | bytes 2654208 | tf_op jit(solution)/shard_map/reduce_scatter | solution.py:372
  700.4 478.8 %reduce-scatter.11.cloned.1.call-start = ((), (), s32[]{:S(2)}) async-start(), calls=%async_computation.9 | async-start | bytes 2654208 | tf_op jit(solution)/shard_map/reduce_scatter | solution.py:371
  712.0 12.2 %copy-start.136 = (f32[768]{0:T(1024)S(1)}, f32[768]{0:T(1024)}, u32[]{:S(2)}) copy-start(f32[768]{0:T(1024)} %get-tuple-element.199) | copy-start | bytes 9220
  712.0 66.7 %copy-start.109 = (f32[768]{0:T(1024)S(1)}, f32[768]{0:T(1024)}, u32[]{:S(2)}) copy-start(f32[768]{0:T(1024)} %copy-done.107) | copy-start | bytes 9220
  757.0 27.3 %copy-start.30 = (s32[256]{0:T(256)S(1)}, s32[256]{0:T(256)}, u32[]{:S(2)}) copy-start(s32[256]{0:T(256)} %get-tuple-element.221) | copy-start | bytes 3076
  1089.9 42.1 %copy-start.111 = (f32[768]{0:T(1024)S(1)}, f32[768]{0:T(1024)}, u32[]{:S(2)}) copy-start(f32[768]{0:T(1024)} %convert_element_type.390) | copy-start | bytes 9220
  1089.9 42.1 %copy-start.116 = (f32[1024]{0:T(1024)S(1)}, f32[1024]{0:T(1024)}, u32[]{:S(2)}) copy-start(f32[1024]{0:T(1024)} %copy-done.115) | copy-start | bytes 12292
  1089.9 42.1 %copy-start.118 = (f32[1024]{0:T(1024)S(1)}, f32[1024]{0:T(1024)}, u32[]{:S(2)}) copy-start(f32[1024]{0:T(1024)} %broadcast_multiply_fusion.10) | copy-start | bytes 12292
  1089.9 42.1 %copy-start.120 = (f32[1024]{0:T(1024)S(1)}, f32[1024]{0:T(1024)}, u32[]{:S(2)}) copy-start(f32[1024]{0:T(1024)} %copy-done.119) | copy-start | bytes 12292
  1089.9 42.1 %copy-start.122 = (f32[1024]{0:T(1024)S(1)}, f32[1024]{0:T(1024)}, u32[]{:S(2)}) copy-start(f32[1024]{0:T(1024)} %copy-done.121) | copy-start | bytes 12292
  1089.9 42.1 %copy-start.138 = (f32[768]{0:T(1024)S(1)}, f32[768]{0:T(1024)}, u32[]{:S(2)}) copy-start(f32[768]{0:T(1024)} %convert_element_type.399) | copy-start | bytes 9220
  1132.0 6.3 copy-start.14
  1132.0 6.3 copy-start.16
  1132.1 6.5 copy-start.36
  (131 other events, 405.0 us)
Sparse Core Ops, SparseCore 0:
  17.9 57.1 all-reduce.29
  207.0 69.8 all-reduce.23
  304.2 68.1 all-reduce.25
  374.1 23.0 all-gather.2
  399.0 24.0 all-gather.4
  443.1 121.4 all-reduce.33
  650.6 128.0 all-reduce.27
  782.2 34.0 reduce-scatter.16
  820.1 40.2 reduce-scatter.14
  862.8 223.8 all-reduce.31
  1090.7 41.8 reduce-scatter.12
  1136.7 42.4 reduce-scatter.10
where the time goes:
time: 1200 us; the launch traced here: 1190 us
  waiting for transfers between devices  594 us (50%)
  other arithmetic  180 us (15%)
  matrix products  160 us (13%)
  blocking collectives  148 us (12%)
  local copies, waits for them, and re-layouts  83.3 us (7%)
  between operations  20.4 us (2%)
    psum x1, waiting for transfers between devices, local(): mlp_sum = lax.psum(mlp_part.astype(jnp.bfloat16), 'mp').astype(jnp.float32)  224 us
    psum x2, waiting for transfers between devices, local(): lax.psum(attn_part.astype(jnp.bfloat16), 'mp').astype(jnp.float32)  117 us
    psum x1, waiting for transfers between devices, local(): lax.psum(hidden_two_part.astype(jnp.bfloat16), 'mp').astype(jnp.float32)  115 us
    unnamed x2, blocking collectives  51.1 us
    unnamed x14, waiting for transfers between devices  43.9 us
    unnamed x405, local copies, waits for them, and re-layouts  40.4 us
    psum x1, blocking collectives, local(): memory_grad, norm_total = lax.psum((memory_part, norm_grads), ('seq', 'mp'))  39.3 us
    another operation x7, other arithmetic, local(): factor = jnp.linalg.cholesky(gram_mat + RIDGE_WEIGHT * identity_mat)  35.2 us
  transfers between devices with their start and end apart: 12, of which 10 were waited for; matrix products, arithmetic and copies ran while one was open for 16% of the time, Pallas kernels for 0%

commit v1 on v0

v1 whole, which is shorter than its diff:
```python
import functools
import math

import jax
import jax.numpy as jnp
from jax import lax
from jax.experimental import pallas as pl
from jax.experimental.pallas import tpu as pltpu
from jax.sharding import PartitionSpec as P

NB = 256
NORM_EPSILON = 1e-05
RIDGE_WEIGHT = 1.0
NARROW_WIDTH = 0.01
BROAD_WIDTH = 0.05
GELU_SCALE = 0.7978845608028654
GELU_CUBIC = 0.044715

BF = jnp.bfloat16
F32 = jnp.float32
HIGHEST = lax.Precision.HIGHEST
BIG_VMEM = 60 * 1024 * 1024


def dot(a, b):
    return jnp.dot(a, b, preferred_element_type=F32)


def dot_nt(a, b):
    return lax.dot_general(a, b, (((1,), (1,)), ((), ())), preferred_element_type=F32)


def dot_tn(a, b, precision=None):
    return lax.dot_general(
        a, b, (((0,), (0,)), ((), ())), preferred_element_type=F32, precision=precision
    )


def norm_parts(values):
    centered = values - jnp.mean(values, axis=-1, keepdims=True)
    inverse = lax.rsqrt(jnp.mean(centered * centered, axis=-1, keepdims=True) + NORM_EPSILON)
    return centered * inverse, inverse


def norm_back(upstream, normed, inverse, gain):
    scaled = upstream * gain
    inner = scaled - jnp.mean(scaled, axis=-1, keepdims=True)
    inner = inner - normed * jnp.mean(scaled * normed, axis=-1, keepdims=True)
    return inner * inverse


def col_sum(values):
    return jnp.sum(values, axis=0, keepdims=True)


def basis_of(places, used):
    column = lax.broadcasted_iota(jnp.int32, (places.shape[0], NB), 1)
    centers = (column.astype(F32) + 0.5) / NB
    widths = jnp.where(column % 2 == 0, NARROW_WIDTH, BROAD_WIDTH).astype(F32)
    scaled = (places - centers) / widths
    return jnp.exp(-0.5 * (scaled * scaled)) * used


def slot_parts(positions, counts, item, total, seg_len):
    places = (item + (positions.astype(F32) + 0.5) / seg_len) / total
    slot = lax.broadcasted_iota(jnp.int32, positions.shape, 0)
    return places, (slot < counts).astype(F32)


def sample_kernel(past_ref, pos_ref, out_ref):
    slots = pos_ref.shape[1]
    seg_len = past_ref.shape[1]
    at = lax.broadcasted_iota(jnp.int32, (slots, seg_len), 1)
    pick = (at == pos_ref[0]).astype(F32).astype(BF)
    out_ref[0] = dot(pick, past_ref[0]).astype(BF)


def sample_rows(past, pos):
    items, seg_len, width = past.shape
    slots = pos.shape[1]
    return pl.pallas_call(
        sample_kernel,
        grid=(items,),
        in_specs=[
            pl.BlockSpec((1, seg_len, width), lambda i: (i, 0, 0)),
            pl.BlockSpec((1, slots, 1), lambda i: (i, 0, 0)),
        ],
        out_specs=pl.BlockSpec((1, slots, width), lambda i: (i, 0, 0)),
        out_shape=jax.ShapeDtypeStruct((items, slots, width), BF),
        name="sample_rows",
    )(past, pos)


def invert_in_place(mat_ref):
    block = 32
    row = lax.broadcasted_iota(jnp.int32, (NB, NB), 0)
    col = lax.broadcasted_iota(jnp.int32, (NB, NB), 1)
    lane = lax.broadcasted_iota(jnp.int32, (block, NB), 1)
    line = lax.broadcasted_iota(jnp.int32, (block, NB), 0)

    def step(_, carry):
        panel = mat_ref[0:block, :]
        for k in range(block):
            pivot_row = panel[k : k + 1, :]
            factor = 1.0 / pivot_row[:, k : k + 1]
            here = lane[0:1] == k
            scaled = jnp.where(here, factor, pivot_row * factor)
            column = panel[:, k : k + 1]
            rest = jnp.where(lane == k, 0.0, panel) - column * scaled
            panel = jnp.where(line == k, scaled, rest)
        mat_ref[0:block, :] = panel
        mat = mat_ref[...]
        inside_row = row < block
        inside_col = col < block
        left = jnp.where(inside_col & ~inside_row, mat, 0.0)
        right = jnp.where(inside_row, mat, 0.0)
        update = jnp.dot(left, right, preferred_element_type=F32, precision=HIGHEST)
        mat = jnp.where(inside_row, mat, jnp.where(inside_col, 0.0, mat) - update)
        mat = pltpu.roll(mat, NB - block, 1)
        mat_ref[0 : NB - block, :] = mat[block:, :]
        mat_ref[NB - block :, :] = mat[:block, :]
        return carry

    lax.fori_loop(0, NB // block, step, 0)


def solve_kernel(sampled_ref, pos_ref, count_ref, coef_ref, inv_ref, mat_ref, mom_ref, *, seg_len):
    total = pos_ref.shape[0]
    slots = pos_ref.shape[1]
    mat_ref[...] = jnp.zeros_like(mat_ref)
    mom_ref[...] = jnp.zeros_like(mom_ref)

    def item(i, carry):
        places, used = slot_parts(pos_ref[i], count_ref[i], i.astype(F32), total, seg_len)
        rows = basis_of(places, used)
        mat_ref[...] += dot_tn(rows, rows, HIGHEST)
        mom_ref[...] += dot_tn(rows, sampled_ref[i].astype(F32), HIGHEST)
        return carry

    lax.fori_loop(0, total, item, 0)
    row = lax.broadcasted_iota(jnp.int32, (NB, NB), 0)
    col = lax.broadcasted_iota(jnp.int32, (NB, NB), 1)
    mat_ref[...] += jnp.where(row == col, RIDGE_WEIGHT, 0.0)
    invert_in_place(mat_ref)
    inverse = mat_ref[...]
    inv_ref[...] = inverse
    coef_ref[...] = jnp.dot(
        inverse, mom_ref[...], preferred_element_type=F32, precision=HIGHEST
    ).astype(BF)


def solve_memory(sampled, pos, counts, seg_len):
    width = sampled.shape[-1]
    return pl.pallas_call(
        functools.partial(solve_kernel, seg_len=seg_len),
        out_shape=(
            jax.ShapeDtypeStruct((NB, width), BF),
            jax.ShapeDtypeStruct((NB, NB), F32),
        ),
        scratch_shapes=[pltpu.VMEM((NB, NB), F32), pltpu.VMEM((NB, width), F32)],
        compiler_params=pltpu.CompilerParams(vmem_limit_bytes=BIG_VMEM),
        name="solve_memory",
    )(sampled, pos, counts)


def past_kernel(
    gmem_ref, coef_ref, vec_ref, inv_ref, pos_ref, count_ref, out_ref, gv_ref, *, total
):
    item_count, slots = pos_ref.shape[0], pos_ref.shape[1]
    seg_len, width = out_ref.shape[1], out_ref.shape[2]
    normed, inverse = norm_parts(coef_ref[...].astype(F32))
    gmem = gmem_ref[...]
    gain = vec_ref[0:1, :]
    coef_grad = norm_back(gmem, normed, inverse, gain)
    gv_ref[...] = jnp.zeros_like(gv_ref)
    gv_ref[0:1, :] = col_sum(gmem * normed)
    gv_ref[1:2, :] = col_sum(gmem)
    features = coef_grad.shape[1]
    part = lax.axis_index("mp")
    row = lax.broadcasted_iota(jnp.int32, (features, width), 0)
    col = lax.broadcasted_iota(jnp.int32, (features, width), 1)
    pick = (row == col + part * width).astype(F32)
    mine = jnp.dot(coef_grad, pick, preferred_element_type=F32, precision=HIGHEST)
    moment = jnp.dot(inv_ref[...], mine, preferred_element_type=F32, precision=HIGHEST)
    first = (lax.axis_index("seq") * item_count).astype(F32)
    at = lax.broadcasted_iota(jnp.int32, (slots, seg_len), 1)
    for i in range(item_count):
        places, used = slot_parts(pos_ref[i], count_ref[i], first + i, total, seg_len)
        rows = basis_of(places, used)
        sampled = jnp.dot(rows, moment, preferred_element_type=F32, precision=HIGHEST)
        spread = (at == pos_ref[i]).astype(F32)
        out_ref[i] = dot_tn(spread, sampled, HIGHEST)


def past_grads(gmem, coef, vec, inv, pos, counts, total, seg_len, width):
    return pl.pallas_call(
        functools.partial(past_kernel, total=total),
        out_shape=(
            jax.ShapeDtypeStruct((pos.shape[0], seg_len, width), F32),
            jax.ShapeDtypeStruct((8, coef.shape[1]), F32),
        ),
        compiler_params=pltpu.CompilerParams(vmem_limit_bytes=BIG_VMEM),
        name="past_grads",
    )(gmem, coef, vec, inv, pos, counts)


def forward_kernel(
    tok_ref,
    coef_ref,
    vec_ref,
    gvec_ref,
    wa_ref,
    wu_ref,
    wd_ref,
    out_ref,
    res_ref,
    hm_ref,
    h2_ref,
    prob_ref,
    key_ref,
    val_ref,
    query_ref,
    att_ref,
    act_ref,
    slope_ref,
    acc_ref,
    *,
    groups,
    head,
):
    step = pl.program_id(0)
    rows, width = tok_ref.shape
    local = query_ref.shape[2]
    half = rows // 2

    @pl.when(step == 0)
    def _():
        gain, bias = vec_ref[0:1, :], vec_ref[1:2, :]
        normed, _ = norm_parts(coef_ref[...].astype(F32))
        hm_ref[0:NB, :] = (normed * gain + bias).astype(BF)
        normed, _ = norm_parts(tok_ref[...].astype(F32))
        hm_ref[NB:, :] = (normed * gain + bias).astype(BF)
        acc_ref[...] = jnp.zeros_like(acc_ref)

    @pl.when(step < groups)
    def _():
        weights = wa_ref[0, 0]
        projected = dot(hm_ref[...], weights[:, : 3 * local]) + gvec_ref[0, 0:1, : 3 * local]
        query = projected[NB:, :local].astype(BF)
        keys = projected[:, local : 2 * local].astype(BF)
        values = projected[:, 2 * local :].astype(BF)
        query_ref[0] = query
        key_ref[0] = keys
        val_ref[0] = values
        query_t = query.T * BF(1.0 / math.sqrt(head))
        value_t = values.T
        line = lax.broadcasted_iota(jnp.int32, (local, rows), 0)
        for h in range(local // head):
            own = (line >= h * head) & (line < (h + 1) * head)
            masked = jnp.where(own, query_t, BF(0.0))
            value_h = value_t[h * head : (h + 1) * head, :]
            for b in range(2):
                span = NB + (b + 1) * half
                scores = dot(keys[:span, :], masked[:, b * half : (b + 1) * half])
                key_at = lax.broadcasted_iota(jnp.int32, (half, half), 0)
                row_at = lax.broadcasted_iota(jnp.int32, (half, half), 1)
                edge = jnp.where(key_at <= row_at, scores[span - half :, :], -1e30)
                scores = jnp.concatenate([scores[: span - half, :], edge], axis=0)
                scores = jnp.exp(scores - jnp.max(scores, axis=0, keepdims=True))
                probs = (scores * (1.0 / jnp.sum(scores, axis=0, keepdims=True))).astype(BF)
                prob_ref[0, h, 0:span, b * half : (b + 1) * half] = probs
                att_ref[0, h * head : (h + 1) * head, b * half : (b + 1) * half] = dot(
                    value_h[:, :span], probs
                ).astype(BF)
        attended = att_ref[0].T
        acc_ref[...] += dot_nt(attended, weights[:, 3 * local :])

    @pl.when(step == groups)
    def _():
        residual = tok_ref[...].astype(F32) + acc_ref[...] + vec_ref[4:5, :]
        res_ref[...] = residual
        normed, _ = norm_parts(residual)
        h2_ref[...] = (normed * vec_ref[2:3, :] + vec_ref[3:4, :]).astype(BF)
        acc_ref[...] = jnp.zeros_like(acc_ref)

    @pl.when(step >= groups)
    def _():
        pre = dot(h2_ref[...], wu_ref[0, 0]) + gvec_ref[0, 1:2, :]
        square = pre * pre
        inner = jnp.tanh(GELU_SCALE * (pre + GELU_CUBIC * pre * square))
        half_up = 0.5 * (1.0 + inner)
        act = (pre * half_up).astype(BF)
        act_ref[0] = act
        slope = GELU_SCALE * (1.0 + 3.0 * GELU_CUBIC * square)
        slope_ref[0] = (half_up + 0.5 * pre * (1.0 - inner * inner) * slope).astype(BF)
        acc_ref[...] += dot_nt(act, wd_ref[0, 0])

    @pl.when(step == 2 * groups - 1)
    def _():
        out_ref[...] = (res_ref[...] + acc_ref[...] + vec_ref[5:6, :]).astype(BF)


def forward_pass(tok, coef, vec, gvec, wide, head):
    rows, width = tok.shape
    groups = wide.shape[0]
    local = width // groups
    hidden = wide.shape[3]
    heads = local // head
    keyed = NB + rows
    first = lambda i: jnp.minimum(i, groups - 1)
    second = lambda i: jnp.maximum(i - groups, 0)
    whole = lambda shape: pl.BlockSpec(shape, lambda i: (0,) * len(shape))
    return pl.pallas_call(
        functools.partial(forward_kernel, groups=groups, head=head),
        grid=(2 * groups,),
        in_specs=[
            whole((rows, width)),
            whole((NB, width)),
            whole((8, width)),
            pl.BlockSpec((1, 8, width), lambda i: (i % groups, 0, 0)),
            pl.BlockSpec((1, 1, width, width), lambda i: (first(i), 0, 0, 0)),
            pl.BlockSpec((1, 1, width, hidden), lambda i: (second(i), 1, 0, 0)),
            pl.BlockSpec((1, 1, width, hidden), lambda i: (second(i), 2, 0, 0)),
        ],
        out_specs=[
            whole((rows, width)),
            whole((rows, width)),
            whole((keyed, width)),
            whole((rows, width)),
            pl.BlockSpec((1, heads, keyed, rows), lambda i: (first(i), 0, 0, 0)),
            pl.BlockSpec((1, keyed, local), lambda i: (first(i), 0, 0)),
            pl.BlockSpec((1, keyed, local), lambda i: (first(i), 0, 0)),
            pl.BlockSpec((1, rows, local), lambda i: (first(i), 0, 0)),
            pl.BlockSpec((1, local, rows), lambda i: (first(i), 0, 0)),
            pl.BlockSpec((1, rows, hidden), lambda i: (second(i), 0, 0)),
            pl.BlockSpec((1, rows, hidden), lambda i: (second(i), 0, 0)),
        ],
        out_shape=[
            jax.ShapeDtypeStruct((rows, width), BF),
            jax.ShapeDtypeStruct((rows, width), F32),
            jax.ShapeDtypeStruct((keyed, width), BF),
            jax.ShapeDtypeStruct((rows, width), BF),
            jax.ShapeDtypeStruct((groups, heads, keyed, rows), BF),
            jax.ShapeDtypeStruct((groups, keyed, local), BF),
            jax.ShapeDtypeStruct((groups, keyed, local), BF),
            jax.ShapeDtypeStruct((groups, rows, local), BF),
            jax.ShapeDtypeStruct((groups, local, rows), BF),
            jax.ShapeDtypeStruct((groups, rows, hidden), BF),
            jax.ShapeDtypeStruct((groups, rows, hidden), BF),
        ],
        scratch_shapes=[pltpu.VMEM((rows, width), F32)],
        compiler_params=pltpu.CompilerParams(vmem_limit_bytes=BIG_VMEM),
        name="forward_pass",
    )(tok, coef, vec, gvec, wide, wide, wide)


def backward_kernel(
    tok_ref,
    cot_ref,
    res_ref,
    vec_ref,
    hm_ref,
    h2_ref,
    prob_ref,
    key_ref,
    val_ref,
    query_ref,
    att_ref,
    act_ref,
    slope_ref,
    wa_ref,
    wu_ref,
    wd_ref,
    tg_ref,
    gmem_ref,
    gmlp_ref,
    gatt_ref,
    gv_ref,
    ggv_ref,
    acc_ref,
    hmt_ref,
    h2t_ref,
    cott_ref,
    gres_ref,
    proj_ref,
    *,
    groups,
    head,
):
    step = pl.program_id(0)
    rows, width = tok_ref.shape
    local = query_ref.shape[2]
    half = rows // 2

    @pl.when(step == 0)
    def _():
        acc_ref[...] = jnp.zeros_like(acc_ref)
        h2t_ref[...] = h2_ref[...].T
        cott_ref[...] = cot_ref[...].T
        gv_ref[...] = jnp.zeros_like(gv_ref)

    @pl.when(step < groups)
    def _():
        upstream = cot_ref[...]
        grad = (dot(upstream, wd_ref[0, 0]) * slope_ref[0].astype(F32)).astype(BF)
        gmlp_ref[0, 1] = dot(cott_ref[...], act_ref[0]).astype(BF)
        gmlp_ref[0, 0] = dot(h2t_ref[...], grad).astype(BF)
        ggv_ref[0] = jnp.zeros_like(ggv_ref[0])
        ggv_ref[0, 0:1, :] = col_sum(grad.astype(F32))
        acc_ref[NB:, :] += dot_nt(grad, wu_ref[0, 0])

    @pl.when(step == groups)
    def _():
        upstream = cot_ref[...].astype(F32)
        normed, inverse = norm_parts(res_ref[...])
        grad = acc_ref[NB:, :]
        g_res = upstream + norm_back(grad, normed, inverse, vec_ref[2:3, :])
        gres_ref[...] = g_res
        g_attn = g_res.astype(BF)
        gv_ref[2:3, :] = col_sum(grad * normed)
        gv_ref[3:4, :] = col_sum(grad)
        gv_ref[4:5, :] = col_sum(g_attn.astype(F32))
        gv_ref[5:6, :] = col_sum(upstream)
        cott_ref[...] = g_attn.T
        h2t_ref[...] = h2t_ref[...]
        hmt_ref[...] = hm_ref[...].T
        acc_ref[...] = jnp.zeros_like(acc_ref)
        proj_ref[0:NB, :] = jnp.zeros((NB, proj_ref.shape[1]), BF)

    @pl.when(step >= groups)
    def _():
        weights = wa_ref[0, 0]
        g_attn = gres_ref[...].astype(BF)
        g_att = dot(g_attn, weights[:, 3 * local :]).astype(BF)
        g_att_t = g_att.T
        att_t = att_ref[0]
        product = g_att_t.astype(F32) * att_t.astype(F32)
        keys, values, query = key_ref[0], val_ref[0], query_ref[0]
        key_t = keys.T
        scale = 1.0 / math.sqrt(head)
        line = lax.broadcasted_iota(jnp.int32, (local, rows), 0)
        lane = lax.broadcasted_iota(jnp.int32, (rows, local), 1)
        key_grad = [jnp.zeros((NB + rows - half, local), F32), jnp.zeros((half, local), F32)]
        val_grad = [jnp.zeros((NB + rows - half, local), F32), jnp.zeros((half, local), F32)]
        query_grads = []
        for h in range(local // head):
            own_t = (line >= h * head) & (line < (h + 1) * head)
            own = (lane >= h * head) & (lane < (h + 1) * head)
            grad_t = jnp.where(own_t, g_att_t, BF(0.0))
            grad_h = jnp.where(own, g_att, BF(0.0))
            query_h = jnp.where(own, query, BF(0.0))
            inner = jnp.sum(product[h * head : (h + 1) * head, :], axis=0, keepdims=True)
            key_h = key_t[h * head : (h + 1) * head, :]
            parts = []
            for b in range(2):
                span = NB + (b + 1) * half
                cols = slice(b * half, (b + 1) * half)
                probs = prob_ref[0, h, 0:span, cols]
                dprob = dot(values[:span, :], grad_t[:, cols])
                dscore = (probs.astype(F32) * (dprob - inner[:, cols])).astype(BF)
                parts.append(dot(key_h[:, :span], dscore))
                val_part = dot(probs, grad_h[cols, :])
                key_part = dot(dscore, query_h[cols, :])
                low = NB + rows - half
                val_grad[0] = val_grad[0] + val_part[:low, :]
                key_grad[0] = key_grad[0] + key_part[:low, :]
                if b == 1:
                    val_grad[1] = val_grad[1] + val_part[low:, :]
                    key_grad[1] = key_grad[1] + key_part[low:, :]
            query_grads.append(jnp.concatenate(parts, axis=1))
        query_grad = (jnp.concatenate(query_grads, axis=0) * scale).astype(BF).T
        key_grad = (jnp.concatenate(key_grad, axis=0) * scale).astype(BF)
        val_sum = jnp.concatenate(val_grad, axis=0)
        val_grad = val_sum.astype(BF)
        proj_ref[NB:, 0:local] = query_grad
        proj_ref[:, local : 2 * local] = key_grad
        proj_ref[:, 2 * local :] = val_grad
        proj = proj_ref[...]
        ggv_ref[0] = jnp.zeros_like(ggv_ref[0])
        ggv_ref[0, 0:1, 0 : 3 * local] = col_sum(proj.astype(F32))
        gatt_ref[0, :, 0 : 3 * local] = dot(hmt_ref[...], proj).astype(BF)
        gatt_ref[0, :, 3 * local :] = dot_nt(cott_ref[...], att_t).astype(BF)
        acc_ref[...] += dot_nt(proj, weights[:, : 3 * local])

    @pl.when(step == 2 * groups - 1)
    def _():
        gmem_ref[...] = acc_ref[0:NB, :]
        grad = acc_ref[NB:, :]
        normed, inverse = norm_parts(tok_ref[...].astype(F32))
        part = norm_back(grad, normed, inverse, vec_ref[0:1, :])
        tg_ref[...] = (gres_ref[...] + part).astype(BF)
        gv_ref[0:1, :] = col_sum(grad * normed)
        gv_ref[1:2, :] = col_sum(grad)


def backward_pass(tok, cot, vec, saved, wide, head):
    res, hm, h2, prob, keys, vals, query, att, act, slope = saved
    rows, width = tok.shape
    groups = wide.shape[0]
    local = width // groups
    hidden = wide.shape[3]
    heads = local // head
    keyed = NB + rows
    first = lambda i: jnp.minimum(i, groups - 1)
    second = lambda i: jnp.maximum(i - groups, 0)
    whole = lambda shape: pl.BlockSpec(shape, lambda i: (0,) * len(shape))
    return pl.pallas_call(
        functools.partial(backward_kernel, groups=groups, head=head),
        grid=(2 * groups,),
        in_specs=[
            whole((rows, width)),
            whole((rows, width)),
            whole((rows, width)),
            whole((8, width)),
            whole((keyed, width)),
            whole((rows, width)),
            pl.BlockSpec((1, heads, keyed, rows), lambda i: (second(i), 0, 0, 0)),
            pl.BlockSpec((1, keyed, local), lambda i: (second(i), 0, 0)),
            pl.BlockSpec((1, keyed, local), lambda i: (second(i), 0, 0)),
            pl.BlockSpec((1, rows, local), lambda i: (second(i), 0, 0)),
            pl.BlockSpec((1, local, rows), lambda i: (second(i), 0, 0)),
            pl.BlockSpec((1, rows, hidden), lambda i: (first(i), 0, 0)),
            pl.BlockSpec((1, rows, hidden), lambda i: (first(i), 0, 0)),
            pl.BlockSpec((1, 1, width, width), lambda i: (second(i), 0, 0, 0)),
            pl.BlockSpec((1, 1, width, hidden), lambda i: (first(i), 1, 0, 0)),
            pl.BlockSpec((1, 1, width, hidden), lambda i: (first(i), 2, 0, 0)),
        ],
        out_specs=[
            whole((rows, width)),
            whole((NB, width)),
            pl.BlockSpec((1, 2, width, hidden), lambda i: (first(i), 0, 0, 0)),
            pl.BlockSpec((1, width, width), lambda i: (second(i), 0, 0)),
            whole((8, width)),
            pl.BlockSpec((1, 8, hidden), lambda i: (i, 0, 0)),
        ],
        out_shape=[
            jax.ShapeDtypeStruct((rows, width), BF),
            jax.ShapeDtypeStruct((NB, width), F32),
            jax.ShapeDtypeStruct((groups, 2, width, hidden), BF),
            jax.ShapeDtypeStruct((groups, width, width), BF),
            jax.ShapeDtypeStruct((8, width), F32),
            jax.ShapeDtypeStruct((2 * groups, 8, hidden), F32),
        ],
        scratch_shapes=[
            pltpu.VMEM((keyed, width), F32),
            pltpu.VMEM((width, keyed), BF),
            pltpu.VMEM((width, rows), BF),
            pltpu.VMEM((width, rows), BF),
            pltpu.VMEM((rows, width), F32),
            pltpu.VMEM((keyed, 3 * local), BF),
        ],
        compiler_params=pltpu.CompilerParams(vmem_limit_bytes=BIG_VMEM),
        name="backward_pass",
    )(
        tok, cot, res, vec, hm, h2, prob, keys, vals, query, att, act, slope, wide, wide, wide
    )


def local(
    tokens,
    cotangent,
    past_state,
    positions,
    counts,
    ln1_gain,
    ln1_bias,
    w_qkv,
    b_qv,
    w_out,
    b_out,
    ln2_gain,
    ln2_bias,
    w_up,
    b_up,
    w_down,
    b_down,
):
    seq, mp = lax.axis_size("seq"), lax.axis_size("mp")
    mp_index = lax.axis_index("mp")
    both = ("seq", "mp")
    item_count, seg_len, local_width = past_state.shape
    slots = positions.shape[1]
    total = item_count * seq
    width = tokens.shape[1]
    part = width // seq
    heads_local = b_qv.shape[1]
    piece = b_qv.shape[2]
    head = piece * seq
    hidden = w_up.shape[1]
    rows = tokens.shape[0] // mp

    pos3 = positions.reshape(item_count, slots, 1)
    counts3 = counts.reshape(item_count, 1, 1)
    sampled = sample_rows(past_state, pos3)
    all_sampled = lax.all_gather(sampled, "seq", axis=0, tiled=True)
    all_pos = lax.all_gather(positions, "seq", axis=0, tiled=True).reshape(total, slots, 1)
    all_counts = lax.all_gather(counts, "seq", axis=0, tiled=True).reshape(total, 1, 1)
    coef_part, inverse = solve_memory(all_sampled, all_pos, all_counts, seg_len)
    coef = lax.all_gather(coef_part, "mp", axis=1, tiled=True)

    shard = jnp.stack(
        [jnp.concatenate([w_qkv[0], w_qkv[1], w_qkv[2], w_out.T], axis=1), w_up, w_down.T]
    )
    wide = lax.all_gather(lax.all_gather(shard, "seq", axis=1, tiled=True), "mp", axis=0)
    small = jnp.concatenate(
        [ln1_gain, ln1_bias, ln2_gain, ln2_bias, b_out, b_down, b_qv.reshape(-1), b_up.reshape(-1)]
    )
    small = lax.all_gather(lax.all_gather(small, "seq", axis=0), "mp", axis=0)
    vec = small[0, :, : 6 * part].reshape(seq, 6, part).transpose(1, 0, 2).reshape(6, width)
    vec = jnp.concatenate([vec, jnp.zeros((2, width), BF)]).astype(F32)
    at = 6 * part
    size = 2 * heads_local * piece
    bias_qv = small[:, :, at : at + size].reshape(mp, seq, 2, heads_local, piece)
    bias_qv = bias_qv.transpose(0, 2, 3, 1, 4).reshape(mp, 2, local_width)
    bias_up = small[:, :, at + size :].reshape(mp, seq, -1, piece)
    bias_up = bias_up.transpose(0, 2, 1, 3).reshape(mp, hidden)
    zero = jnp.zeros((mp, local_width), BF)
    first = jnp.concatenate([bias_qv[:, 0], zero, bias_qv[:, 1], zero], axis=1)
    gvec = jnp.concatenate(
        [first[:, None], bias_up[:, None], jnp.zeros((mp, 6, width), BF)], axis=1
    ).astype(F32)

    tok = lax.dynamic_slice_in_dim(tokens, mp_index * rows, rows, 0)
    cot = lax.dynamic_slice_in_dim(cotangent, mp_index * rows, rows, 0)
    forward = forward_pass(tok, coef, vec, gvec, wide, head)
    block_out = lax.all_gather(forward[0], "mp", axis=0, tiled=True)
    tok_grad, gmem, g_mlp, g_att, gv, ggv = backward_pass(tok, cot, vec, forward[1:], wide, head)
    block_grad = lax.all_gather(tok_grad, "mp", axis=0, tiled=True)

    gmem, gv, ggv = lax.psum((gmem, gv, ggv), both)
    past_grad, gv_mem = past_grads(
        gmem, coef, vec, inverse, pos3, counts3, total, seg_len, local_width
    )
    gv = gv + gv_mem

    grads = jnp.concatenate([g_att[:, None], g_mlp], axis=1)
    grads = lax.psum_scatter(grads, "mp", scatter_dimension=0, tiled=False)
    grads = lax.psum_scatter(grads, "seq", scatter_dimension=1, tiled=True).astype(F32)
    attn = grads[0]
    qkv_grad = jnp.stack([attn[:, i * local_width : (i + 1) * local_width] for i in range(3)])
    out_grad = attn[:, 3 * local_width :].T
    seq_index = lax.axis_index("seq")
    vec_own = lax.dynamic_slice_in_dim(gv, seq_index * part, part, 1)
    qv = lax.dynamic_slice_in_dim(ggv, mp + mp_index, 1, 0)[0, 0]
    qv = jnp.stack([qv[:local_width], qv[2 * local_width : 3 * local_width]])
    qv = qv.reshape(2, heads_local, head)
    qv = lax.dynamic_slice_in_dim(qv, seq_index * piece, piece, 2)
    up = lax.dynamic_slice_in_dim(ggv, mp_index, 1, 0)[0, 0].reshape(-1, head)
    up = lax.dynamic_slice_in_dim(up, seq_index * piece, piece, 1)
    return (
        block_out,
        block_grad,
        past_grad,
        vec_own[0],
        vec_own[1],
        qkv_grad,
        qv,
        out_grad,
        vec_own[4],
        vec_own[2],
        vec_own[3],
        grads[1],
        up,
        grads[2].T,
        vec_own[5],
    )


def solution(mesh):
    row = P("seq", None)
    placed = (
        row,
        row,
        P("seq", None, "mp"),
        row,
        P("seq"),
        P("seq"),
        P("seq"),
        P(None, "seq", "mp"),
        P(None, "mp", "seq"),
        P("mp", "seq"),
        P("seq"),
        P("seq"),
        P("seq"),
        P("seq", "mp"),
        P("mp", "seq"),
        P("mp", "seq"),
        P("seq"),
    )
    return jax.shard_map(
        local,
        mesh=mesh,
        in_specs=placed,
        out_specs=(row, row, placed[2]) + placed[5:],
        check_vma=False,
    )
```

time: 1200 us -> 960 us (0.80); the launches traced: 1190 us -> 959 us
  other arithmetic: 180 us -> 18.7 us
  matrix products: 160 us -> 0 us
  Pallas kernels: 0 us -> 126 us
  local copies, waits for them, and re-layouts: 83.3 us -> 33.4 us
  waiting for transfers between devices: 594 us -> 621 us
    psum x6 -> x1, waiting for transfers between devices: 478 us -> 93.3 us  [local(): gmem, gv, ggv = lax.psum((gmem, gv, ggv), both)]
    reduce_scatter x2, waiting for transfers between devices: 34.3 us -> 284 us  [the longest x1 234 us: local(): grads = lax.psum_scatter(grads, 'mp', scatter_dimension=0, tiled=False)]
    all_gather x2 -> x4, waiting for transfers between devices: 37.1 us -> 241 us  [the longest x1 88.9 us: local(): lax.all_gather(lax.all_gather(shard, 'seq', axis=1, tiled=True), 'mp', ax...]
    dot_general x69 -> x0, matrix products: 153 us -> none  [the longest x2 12 us: attend_back(): jnp.einsum('ghlm,glhe->gmhe', window_probs.astype(jnp.bfloat16), out_grad...]
    pallas_call x0 -> x5, Pallas kernels: none -> 126 us  [the longest x1 44 us: backward_pass(): pl.pallas_call(functools.partial(backward_kernel, groups=groups, head=hea...]
    another operation x11 -> x4, other arithmetic: 57.2 us -> 2.71 us  [the longest x2 1.9 us: local(): jnp.stack([jnp.concatenate([w_qkv[0], w_qkv[1], w_qkv[2], w_out.T], axis=...]
    unnamed x14 -> x7, waiting for transfers between devices: 43.9 us -> 1.64 us
    reduce_sum x19 -> x0, other arithmetic: 41.7 us -> none  [the longest x2 6.96 us: attend(): total = jnp.sum(jnp.exp(window - largest), axis=-1, keepdims=True)]
  transfers between devices with their start and end apart: 12 -> 7, of which waited for: 10 -> 7; matrix products, arithmetic and copies ran while one was open for 16% -> 3% of each run, Pallas kernels for 0% -> 5%
where the time goes in v1:
time: 960 us; the launch traced here: 959 us
  waiting for transfers between devices  621 us (65%)
  blocking collectives  144 us (15%)
  Pallas kernels  126 us (13%)
  local copies, waits for them, and re-layouts  33.4 us (3%)
  other arithmetic  18.7 us (2%)
  between operations  15.8 us (2%)
    reduce_scatter x1, waiting for transfers between devices, local(): grads = lax.psum_scatter(grads, 'mp', scatter_dimension=0, tiled=False)  234 us
    psum x1, waiting for transfers between devices, local(): gmem, gv, ggv = lax.psum((gmem, gv, ggv), both)  93.3 us
    all_gather x1, waiting for transfers between devices, local(): lax.all_gather(lax.all_gather(shard, 'seq', axis=1, tiled=True), 'mp', ax...  88.9 us
    all_gather x1, waiting for transfers between devices, local(): block_out = lax.all_gather(forward[0], 'mp', axis=0, tiled=True)  63.7 us
    all_gather x1, waiting for transfers between devices, local(): block_grad = lax.all_gather(tok_grad, 'mp', axis=0, tiled=True)  51.6 us
    reduce_scatter x1, waiting for transfers between devices, local(): lax.psum_scatter(grads, 'seq', scatter_dimension=1, tiled=True).astype(F32)  50.7 us
    pallas_call x1, Pallas kernels, backward_pass(): pl.pallas_call(functools.partial(backward_kernel, groups=groups, head=hea...  44 us
    psum x1, blocking collectives, local(): gmem, gv, ggv = lax.psum((gmem, gv, ggv), both)  41.9 us
  transfers between devices with their start and end apart: 7, of which 7 were waited for; matrix products, arithmetic and copies ran while one was open for 3% of the time, Pallas kernels for 5%

profile of v1, /device:TPU:0, one launch (start us, length us, event | category | flops | bytes accessed | tf_op | source)
XLA Modules:
  0.0 958.7 jit_solution(17751088968712292536)
XLA Ops:
  7.3 1.0 slice_bitcast_fusion.9
  8.4 0.9 copy.134
  9.3 0.1 maximum_bitcast_fusion
  9.4 1.8 pad_maximum_fusion.1
  11.2 36.8 %all-gather.9.cloned.1.call-done = bf16[3,768,768]{2,1,0:T(8,128)(2,1)} async-done(((bf16[3,96,768]{2,1,0:T(8,128)(2,1)}), bf16[3,768,768]{2,1,0:T(8,128)(2,1)}) %all-gather.9.cloned.1.call-update) | async-done | bytes 3538960 | tf_op jit(solution)/shard_map/all_gather | solution.py:604
  48.1 0.6 dynamic-slice
  49.4 0.2 dynamic-update-slice
  49.6 7.2 all-reduce.1
  57.6 0.1 reshape.73
  57.9 0.2 dynamic-update-slice.1
  58.2 23.5 %all-reduce.2 = bf16[5760]{0:T(1024)(128)(2,1)S(1)} all-reduce(bf16[5760]{0:T(1024)(128)(2,1)S(1)} %dynamic-update-slice.1), channel_id=2, replica_groups=mesh['seq'=8,'mp'=4] {'seq'}, use_global_device_ids=true, to_apply=%add.2 | all-reduce | flops 5760 | bytes 23040
  81.7 0.1 reshape.79
  81.8 22.4 %all-gather.1 = bf16[32,720]{1,0:T(8,128)(2,1)S(1)} all-gather(bf16[8,720]{1,0:T(8,128)(2,1)S(1)} %reshape.79), channel_id=3, replica_groups=mesh['seq'=8,'mp'=4] {'mp'}, dimensions={0}, use_global_device_ids=true | all-gather | bytes 57600 | tf_op jit(solution)/shard_map/all_gather | solution.py:608
  104.3 0.1 reshape.75
  104.4 0.1 reshape.76
  104.6 0.6 copy.132
  105.3 0.2 reshape.77
  105.4 0.7 broadcast_in_dim_reshape.4
  106.4 0.7 copy.125.count_ref
  107.1 0.8 copy.121.pos_ref
  107.9 2.0 copy.120.past_ref
  109.9 2.1 sample_rows.1
  111.9 1.0 copy.122
  112.9 11.4 %all_gather.39 = bf16[16,128,192]{1,2,0:T(8,128)(2,1)} all-gather(bf16[2,128,192]{1,2,0:T(8,128)(2,1)S(1)} %copy.122), channel_id=1, replica_groups=mesh['seq'=8,'mp'=4] {'seq'}, dimensions={0}, use_global_device_ids=true | all-gather | bytes 884736 | tf_op jit(solution)/shard_map/all_gather | solution.py:595
  124.4 2.2 copy.123.sampled_ref
  126.6 8.7 all-gather.3
  135.3 1.3 copy.124.pos_ref
  136.7 38.8 %solve_memory.1 = (bf16[256,192]{1,0:T(8,128)(2,1)}, f32[256,256]{1,0:T(8,128)}) custom-call(bf16[16,128,192]{2,1,0:T(8,128)(2,1)} %copy.123.sampled_ref, s32[16,128,1]{2,1,0:T(8,128)} %copy.124.pos_ref, s32[16,1,1]{2,1,0:T(1,128)} %copy.125.count_ref), custom_call_target="tpu_custom_call" | custom-call | tf_op jit(solution)/shard_map/solve_memory/pallas_call | solution.py:154
  175.5 1.6 copy.126
  177.1 29.1 %all_gather.42 = bf16[256,768]{0,1:T(8,128)(2,1)S(1)} all-gather(bf16[256,192]{0,1:T(8,128)(2,1)} %copy.126), channel_id=1, replica_groups=mesh['seq'=8,'mp'=4] {'mp'}, dimensions={1}, use_global_device_ids=true | all-gather | bytes 491520 | tf_op jit(solution)/shard_map/all_gather | solution.py:599
  206.2 0.9 copy.135.coef_ref
  207.2 0.6 pad_convert_fusion.vec_ref
  207.9 0.9 constant_dynamic-slice_fusion.4.tok_ref
  208.8 2.1 constant_dynamic-slice_fusion.3.cot_ref
  210.9 0.7 maximum_convert_fusion.gvec_ref
  211.6 88.9 %all-gather.15.cloned.1.call-done = bf16[12,768,768]{2,1,0:T(8,128)(2,1)} async-done(((bf16[3,768,768]{2,1,0:T(8,128)(2,1)}), bf16[12,768,768]{2,1,0:T(8,128)(2,1)}) %all-gather.15.cloned.1.call-update) | async-done | bytes 14155792 | tf_op jit(solution)/shard_map/all_gather | solution.py:604
  300.6 34.4 %forward_pass.1 = (bf16[512,768]{1,0:T(8,128)(2,1)}, f32[512,768]{1,0:T(8,128)}, bf16[768,768]{1,0:T(8,128)(2,1)}, bf16[512,768]{1,0:T(8,128)(2,1)}, bf16[4,3,76...) custom-call(bf16[512,768]{1,0:T(8,128)(2,1)} %constant_dynamic-slice, ...), custom_call_target="tpu_custom_call" | custom-call | tf_op jit(solution)/shard_map/forward_pass/pallas_call | solution.py:313
  335.0 44.0 %backward_pass.1 = (bf16[512,768]{1,0:T(8,128)(2,1)}, f32[256,768]{1,0:T(8,128)}, bf16[4,2,768,768]{3,2,1,0:T(8,128)(2,1)}, bf16[4,768,768]{2,1,0:T(8,128)(2,1)}...) custom-call(bf16[512,768]{1,0:T(8,128)(2,1)} %constant_dynamic-slice_fusion.4.tok_ref, ...), custom_call_target="tpu_custom_call" | custom-call | tf_op jit(solution)/shard_map/backward_pass/pallas_call | solution.py:507
  379.0 12.7 %pad_maximum_fusion = bf16[4,3,768,768]{3,2,1,0:T(8,128)(2,1)} fusion(bf16[4,2,768,768]{3,2,1,0:T(8,128)(2,1)} %get-tuple-element.55, bf16[4,1,768,768]{3,2,1,0:T(8,128)(2,1)} %bitcast.73), kind=kLoop, calls=%fused_computation | loop fusion | flops 7077888 | bytes 28311552 | tf_op jit(solution)/shard_map/concatenate | solution.py:636
  391.8 0.5 all-reduce.6.cloned.1.call-update
  392.3 0.5 all-gather.13.cloned.1.call-update
  392.9 0.5 all-gather.11.cloned.1.call-update
  393.5 233.8 %reduce-scatter.3.cloned.1.call-done = bf16[1,3,768,768]{3,2,1,0:T(8,128)(2,1)} async-done(((bf16[4,3,768,768]{3,2,1,0:T(8,128)(2,1)}), bf16[1,3,768,768]{3,2,1,0:T(8,128)(2,1)}) %reduce-scatter.3.cloned.1.call-update) | async-done | bytes 3538960 | tf_op jit(solution)/shard_map/reduce_scatter | solution.py:637
  627.3 0.6 copy.138.count_ref
  628.0 41.9 %psum.22 = f32[8,768]{1,0:T(8,128)S(1)} all-reduce(f32[8,768]{1,0:T(8,128)S(1)} %copy-done.5), channel_id=1, replica_groups=mesh['seq'=8,'mp'=4] {'seq','mp'}, use_global_device_ids=true, to_apply=%region_1.0 | all-reduce | flops 6144 | bytes 49152 | tf_op jit(solution)/shard_map/psum | solution.py:630
  669.9 93.3 %all-reduce.6.cloned.1.call-done = (f32[256,768]{1,0:T(8,128)}, f32[8,8,768]{2,1,0:T(8,128)}) async-done(((f32[256,768]{1,0:T(8,128)}, f32[8,8,768]{2,1,0:T(8,128)}), (f32[256,768]{1,0:T(8,128)}, f32[8,8,768]{2,1,0:T(8,128)})) %all-reduce.6.cloned.1.call-update) | async-done | bytes 983056 | tf_op jit(solution)/shard_map/psum | solution.py:630
  763.2 0.7 fusion.1
  764.2 0.6 copy.142
  764.8 6.5 past_grads.1
  771.3 2.5 copy.141
  773.8 0.8 dynamic-slice_reduce_fusion
  774.7 0.7 copy.146
  775.4 0.8 dynamic-slice_add_fusion
  776.2 0.5 slice_bitcast_fusion.10
  776.7 51.6 %all-gather.13.cloned.1.call-done = bf16[2048,768]{1,0:T(8,128)(2,1)} async-done(((bf16[512,768]{1,0:T(8,128)(2,1)}), bf16[2048,768]{1,0:T(8,128)(2,1)}) %all-gather.13.cloned.1.call-update) | async-done | bytes 3145744 | tf_op jit(solution)/shard_map/all_gather | solution.py:628
  828.3 63.7 %all-gather.11.cloned.1.call-done = bf16[2048,768]{1,0:T(8,128)(2,1)} async-done(((bf16[512,768]{1,0:T(8,128)(2,1)}), bf16[2048,768]{1,0:T(8,128)(2,1)}) %all-gather.11.cloned.1.call-update) | async-done | bytes 3145744 | tf_op jit(solution)/shard_map/all_gather | solution.py:626
  892.0 50.7 %reduce-scatter.5.cloned.1.call-done = bf16[3,96,768]{2,1,0:T(8,128)(2,1)} async-done(((bf16[3,768,768]{2,1,0:T(8,128)(2,1)}), bf16[3,96,768]{2,1,0:T(8,128)(2,1)}) %reduce-scatter.5.cloned.1.call-update) | async-done | bytes 442384 | tf_op jit(solution)/shard_map/reduce_scatter | solution.py:638
  942.7 1.1 convert_element_type.11
  943.8 0.9 slice_bitcast_fusion
  944.6 0.1 slice_bitcast_fusion.3
  944.8 0.7 copy.143
  945.5 0.7 pad_maximum_fusion.2
  946.2 3.9 copy.155
  950.2 1.7 copy.156
  (70 shorter events, 1.6 us)
Async XLA Ops:
  7.2 200.7 %copy-start = (bf16[2048,768]{1,0:T(8,128)(2,1)S(1)}, bf16[2048,768]{1,0:T(8,128)(2,1)}, u32[]{:S(2)}) copy-start(bf16[2048,768]{1,0:T(8,128)(2,1)} %param.17) | copy-start | bytes 9437188
  7.2 40.9 %copy-start.16 = (u32[32]{0:T(128)S(1)}, u32[32]{0:T(128)}, u32[]{:S(2)}) copy-start(u32[32]{0:T(128)} %constant.39) | copy-start | bytes 388
  7.2 42.2 %copy-start.15 = (s32[2]{0:T(128)S(1)}, s32[2]{0:T(128)}, u32[]{:S(2)}) copy-start(s32[2]{0:T(128)} %param.21) | copy-start | bytes 28
  7.2 50.3 %copy-start.7 = (bf16[12,8]{0,1:T(8,128)(2,1)S(1)}, bf16[12,8]{0,1:T(8,128)(2,1)}, u32[]{:S(2)}) copy-start(bf16[12,8]{0,1:T(8,128)(2,1)} %param.31) | copy-start | bytes 580
  7.2 50.4 %copy-start.8 = (bf16[2,3,8]{2,0,1:T(2,128)(2,1)S(1)}, bf16[2,3,8]{2,0,1:T(2,128)(2,1)}, u32[]{:S(2)}) copy-start(bf16[2,3,8]{2,0,1:T(2,128)(2,1)} %param.25) | copy-start | bytes 292
  7.2 50.5 %copy-start.9 = (bf16[96]{0:T(256)(128)(2,1)S(1)}, bf16[96]{0:T(256)(128)(2,1)}, u32[]{:S(2)}) copy-start(bf16[96]{0:T(256)(128)(2,1)} %param.22) | copy-start | bytes 580
  7.3 50.5 %copy-start.10 = (bf16[96]{0:T(256)(128)(2,1)S(1)}, bf16[96]{0:T(256)(128)(2,1)}, u32[]{:S(2)}) copy-start(bf16[96]{0:T(256)(128)(2,1)} %param.23) | copy-start | bytes 580
  7.3 50.5 %copy-start.13 = (bf16[96]{0:T(256)(128)(2,1)S(1)}, bf16[96]{0:T(256)(128)(2,1)}, u32[]{:S(2)}) copy-start(bf16[96]{0:T(256)(128)(2,1)} %param.27) | copy-start | bytes 580
  7.3 50.5 %copy-start.11 = (bf16[96]{0:T(256)(128)(2,1)S(1)}, bf16[96]{0:T(256)(128)(2,1)}, u32[]{:S(2)}) copy-start(bf16[96]{0:T(256)(128)(2,1)} %param.28) | copy-start | bytes 580
  7.3 50.5 %copy-start.12 = (bf16[96]{0:T(256)(128)(2,1)S(1)}, bf16[96]{0:T(256)(128)(2,1)}, u32[]{:S(2)}) copy-start(bf16[96]{0:T(256)(128)(2,1)} %param.29) | copy-start | bytes 580
  7.3 50.5 %copy-start.14 = (bf16[96]{0:T(256)(128)(2,1)S(1)}, bf16[96]{0:T(256)(128)(2,1)}, u32[]{:S(2)}) copy-start(bf16[96]{0:T(256)(128)(2,1)} %param.33) | copy-start | bytes 580
  7.3 40.7 %all-gather.9.cloned.1.call-start = ((), (), s32[]{:S(2)}) async-start(), calls=%async_computation.2 | async-start | bytes 3981312 | tf_op jit(solution)/shard_map/all_gather | solution.py:604
  9.3 97.8 %copy-start.6 = (s32[2,128]{1,0:T(2,128)S(1)}, s32[2,128]{1,0:T(2,128)}, u32[]{:S(2)}) copy-start(s32[2,128]{1,0:T(2,128)} %param.20) | copy-start | bytes 3076
  11.2 289.4 %all-gather.15.cloned.1.call-start = ((), (), s32[]{:S(2)}) async-start(), calls=%async_computation.7 | async-start | bytes 17694720 | tf_op jit(solution)/shard_map/all_gather | solution.py:604
  48.0 579.3 %reduce-scatter.3.cloned.1.call-start = ((), (), s32[]{:S(2)}) async-start(), calls=%async_computation.5 | async-start | bytes 17694720 | tf_op jit(solution)/shard_map/reduce_scatter | solution.py:637
  207.2 3.7 copy-start.3
  207.2 3.7 copy-start.4
  391.7 236.3 %copy-start.5 = (f32[8,768]{1,0:T(8,128)S(1)}, f32[8,768]{1,0:T(8,128)}, u32[]{:S(2)}) copy-start(f32[8,768]{1,0:T(8,128)} %get-tuple-element.52) | copy-start | bytes 73732
  391.7 371.5 %all-reduce.6.cloned.1.call-start = ((), (), s32[]{:S(2)}) async-start(), calls=%async_computation.8 | async-start | bytes 1966080 | tf_op jit(solution)/shard_map/psum | solution.py:630
  392.3 436.1 %all-gather.13.cloned.1.call-start = ((), (), s32[]{:S(2)}) async-start(), calls=%async_computation.4 | async-start | bytes 3932160 | tf_op jit(solution)/shard_map/all_gather | solution.py:628
  392.9 499.2 %all-gather.11.cloned.1.call-start = ((), (), s32[]{:S(2)}) async-start(), calls=%async_computation.3 | async-start | bytes 3932160 | tf_op jit(solution)/shard_map/all_gather | solution.py:626
  393.4 549.3 %reduce-scatter.5.cloned.1.call-start = ((), (), s32[]{:S(2)}) async-start(), calls=%async_computation.6 | async-start | bytes 3981312 | tf_op jit(solution)/shard_map/reduce_scatter | solution.py:638
  946.2 3.9 copy-start.2
  946.2 5.6 copy-start.1
Sparse Core Ops, SparseCore 0:
  11.3 36.6 all-gather.8
  49.6 250.9 all-gather.14
  391.8 235.4 reduce-scatter.2
  633.0 130.1 all-reduce.5
  764.7 63.5 all-gather.12
  829.8 62.1 all-gather.10
  895.9 46.7 reduce-scatter.4

commit v2 on v1

--- a/solution.py
+++ b/solution.py
@@ -59,12 +59,6 @@
     widths = jnp.where(column % 2 == 0, NARROW_WIDTH, BROAD_WIDTH).astype(F32)
     scaled = (places - centers) / widths
     return jnp.exp(-0.5 * (scaled * scaled)) * used
-
-
-def slot_parts(positions, counts, item, total, seg_len):
-    places = (item + (positions.astype(F32) + 0.5) / seg_len) / total
-    slot = lax.broadcasted_iota(jnp.int32, positions.shape, 0)
-    return places, (slot < counts).astype(F32)
 
 
 def sample_kernel(past_ref, pos_ref, out_ref):
@@ -124,20 +118,21 @@
     lax.fori_loop(0, NB // block, step, 0)
 
 
-def solve_kernel(sampled_ref, pos_ref, count_ref, coef_ref, inv_ref, mat_ref, mom_ref, *, seg_len):
-    total = pos_ref.shape[0]
-    slots = pos_ref.shape[1]
+def solve_kernel(sampled_ref, meta_ref, coef_ref, inv_ref, mat_ref, mom_ref, *, items):
+    slots = meta_ref.shape[2]
     mat_ref[...] = jnp.zeros_like(mat_ref)
     mom_ref[...] = jnp.zeros_like(mom_ref)
 
-    def item(i, carry):
-        places, used = slot_parts(pos_ref[i], count_ref[i], i.astype(F32), total, seg_len)
-        rows = basis_of(places, used)
-        mat_ref[...] += dot_tn(rows, rows, HIGHEST)
-        mom_ref[...] += dot_tn(rows, sampled_ref[i].astype(F32), HIGHEST)
+    def owner(s, carry):
+        column = meta_ref[s].T
+        for i in range(items):
+            rows = basis_of(column[:, i : i + 1], column[:, items + i : items + i + 1])
+            mat_ref[...] += dot_tn(rows, rows, HIGHEST)
+            sampled = sampled_ref[s, i * slots : (i + 1) * slots, :]
+            mom_ref[...] += dot_tn(rows, sampled.astype(F32), HIGHEST)
         return carry
 
-    lax.fori_loop(0, total, item, 0)
+    lax.fori_loop(0, meta_ref.shape[0], owner, 0)
     row = lax.broadcasted_iota(jnp.int32, (NB, NB), 0)
     col = lax.broadcasted_iota(jnp.int32, (NB, NB), 1)
     mat_ref[...] += jnp.where(row == col, RIDGE_WEIGHT, 0.0)
@@ -149,10 +144,10 @@
     ).astype(BF)
 
 
-def solve_memory(sampled, pos, counts, seg_len):
+def solve_memory(sampled, meta, items):
     width = sampled.shape[-1]
     return pl.pallas_call(
-        functools.partial(solve_kernel, seg_len=seg_len),
+        functools.partial(solve_kernel, items=items),
         out_shape=(
             jax.ShapeDtypeStruct((NB, width), BF),
             jax.ShapeDtypeStruct((NB, NB), F32),
@@ -160,18 +155,15 @@
         scratch_shapes=[pltpu.VMEM((NB, NB), F32), pltpu.VMEM((NB, width), F32)],
         compiler_params=pltpu.CompilerParams(vmem_limit_bytes=BIG_VMEM),
         name="solve_memory",
-    )(sampled, pos, counts)
-
-
-def past_kernel(
-    gmem_ref, coef_ref, vec_ref, inv_ref, pos_ref, count_ref, out_ref, gv_ref, *, total
-):
+    )(sampled, meta)
+
+
+def past_kernel(gmem_ref, coef_ref, vec_ref, inv_ref, meta_ref, pos_ref, out_ref, gv_ref):
     item_count, slots = pos_ref.shape[0], pos_ref.shape[1]
     seg_len, width = out_ref.shape[1], out_ref.shape[2]
     normed, inverse = norm_parts(coef_ref[...].astype(F32))
     gmem = gmem_ref[...]
-    gain = vec_ref[0:1, :]
-    coef_grad = norm_back(gmem, normed, inverse, gain)
+    coef_grad = norm_back(gmem, normed, inverse, vec_ref[0:1, :])
     gv_ref[...] = jnp.zeros_like(gv_ref)
     gv_ref[0:1, :] = col_sum(gmem * normed)
     gv_ref[1:2, :] = col_sum(gmem)
@@ -182,26 +174,25 @@
     pick = (row == col + part * width).astype(F32)
     mine = jnp.dot(coef_grad, pick, preferred_element_type=F32, precision=HIGHEST)
     moment = jnp.dot(inv_ref[...], mine, preferred_element_type=F32, precision=HIGHEST)
-    first = (lax.axis_index("seq") * item_count).astype(F32)
     at = lax.broadcasted_iota(jnp.int32, (slots, seg_len), 1)
+    column = meta_ref[...].T
     for i in range(item_count):
-        places, used = slot_parts(pos_ref[i], count_ref[i], first + i, total, seg_len)
-        rows = basis_of(places, used)
+        rows = basis_of(column[:, i : i + 1], column[:, item_count + i : item_count + i + 1])
         sampled = jnp.dot(rows, moment, preferred_element_type=F32, precision=HIGHEST)
         spread = (at == pos_ref[i]).astype(F32)
         out_ref[i] = dot_tn(spread, sampled, HIGHEST)
 
 
-def past_grads(gmem, coef, vec, inv, pos, counts, total, seg_len, width):
+def past_grads(gmem, coef, vec, inv, meta, pos, seg_len, width):
     return pl.pallas_call(
-        functools.partial(past_kernel, total=total),
+        past_kernel,
         out_shape=(
             jax.ShapeDtypeStruct((pos.shape[0], seg_len, width), F32),
             jax.ShapeDtypeStruct((8, coef.shape[1]), F32),
         ),
         compiler_params=pltpu.CompilerParams(vmem_limit_bytes=BIG_VMEM),
         name="past_grads",
-    )(gmem, coef, vec, inv, pos, counts)
+    )(gmem, coef, vec, inv, meta, pos)
 
 
 def forward_kernel(
@@ -244,7 +235,7 @@
 
     @pl.when(step < groups)
     def _():
-        weights = wa_ref[0, 0]
+        weights = wa_ref[0]
         projected = dot(hm_ref[...], weights[:, : 3 * local]) + gvec_ref[0, 0:1, : 3 * local]
         query = projected[NB:, :local].astype(BF)
         keys = projected[:, local : 2 * local].astype(BF)
@@ -285,7 +276,7 @@
 
     @pl.when(step >= groups)
     def _():
-        pre = dot(h2_ref[...], wu_ref[0, 0]) + gvec_ref[0, 1:2, :]
+        pre = dot(h2_ref[...], wu_ref[0]) + gvec_ref[0, 1:2, :]
         square = pre * pre
         inner = jnp.tanh(GELU_SCALE * (pre + GELU_CUBIC * pre * square))
         half_up = 0.5 * (1.0 + inner)
@@ -293,7 +284,7 @@
         act_ref[0] = act
         slope = GELU_SCALE * (1.0 + 3.0 * GELU_CUBIC * square)
         slope_ref[0] = (half_up + 0.5 * pre * (1.0 - inner * inner) * slope).astype(BF)
-        acc_ref[...] += dot_nt(act, wd_ref[0, 0])
+        acc_ref[...] += dot_nt(act, wd_ref[0])
 
     @pl.when(step == 2 * groups - 1)
     def _():
@@ -302,9 +293,9 @@
 
 def forward_pass(tok, coef, vec, gvec, wide, head):
     rows, width = tok.shape
-    groups = wide.shape[0]
+    groups = wide[0].shape[0]
     local = width // groups
-    hidden = wide.shape[3]
+    hidden = wide[1].shape[2]
     heads = local // head
     keyed = NB + rows
     first = lambda i: jnp.minimum(i, groups - 1)
@@ -318,9 +309,9 @@
             whole((NB, width)),
             whole((8, width)),
             pl.BlockSpec((1, 8, width), lambda i: (i % groups, 0, 0)),
-            pl.BlockSpec((1, 1, width, width), lambda i: (first(i), 0, 0, 0)),
-            pl.BlockSpec((1, 1, width, hidden), lambda i: (second(i), 1, 0, 0)),
-            pl.BlockSpec((1, 1, width, hidden), lambda i: (second(i), 2, 0, 0)),
+            pl.BlockSpec((1, width, width), lambda i: (first(i), 0, 0)),
+            pl.BlockSpec((1, width, hidden), lambda i: (second(i), 0, 0)),
+            pl.BlockSpec((1, width, hidden), lambda i: (second(i), 0, 0)),
         ],
         out_specs=[
             whole((rows, width)),
@@ -351,7 +342,7 @@
         scratch_shapes=[pltpu.VMEM((rows, width), F32)],
         compiler_params=pltpu.CompilerParams(vmem_limit_bytes=BIG_VMEM),
         name="forward_pass",
-    )(tok, coef, vec, gvec, wide, wide, wide)
+    )(tok, coef, vec, gvec, *wide)
 
 
 def backward_kernel(
@@ -373,7 +364,8 @@
     wd_ref,
     tg_ref,
     gmem_ref,
-    gmlp_ref,
+    gup_ref,
+    gdown_ref,
     gatt_ref,
     gv_ref,
     ggv_ref,
@@ -402,12 +394,12 @@
     @pl.when(step < groups)
     def _():
         upstream = cot_ref[...]
-        grad = (dot(upstream, wd_ref[0, 0]) * slope_ref[0].astype(F32)).astype(BF)
-        gmlp_ref[0, 1] = dot(cott_ref[...], act_ref[0]).astype(BF)
-        gmlp_ref[0, 0] = dot(h2t_ref[...], grad).astype(BF)
+        grad = (dot(upstream, wd_ref[0]) * slope_ref[0].astype(F32)).astype(BF)
+        gdown_ref[0] = dot(cott_ref[...], act_ref[0]).astype(BF)
+        gup_ref[0] = dot(h2t_ref[...], grad).astype(BF)
         ggv_ref[0] = jnp.zeros_like(ggv_ref[0])
         ggv_ref[0, 0:1, :] = col_sum(grad.astype(F32))
-        acc_ref[NB:, :] += dot_nt(grad, wu_ref[0, 0])
+        acc_ref[NB:, :] += dot_nt(grad, wu_ref[0])
 
     @pl.when(step == groups)
     def _():
@@ -422,14 +414,13 @@
         gv_ref[4:5, :] = col_sum(g_attn.astype(F32))
         gv_ref[5:6, :] = col_sum(upstream)
         cott_ref[...] = g_attn.T
-        h2t_ref[...] = h2t_ref[...]
         hmt_ref[...] = hm_ref[...].T
         acc_ref[...] = jnp.zeros_like(acc_ref)
         proj_ref[0:NB, :] = jnp.zeros((NB, proj_ref.shape[1]), BF)
 
     @pl.when(step >= groups)
     def _():
-        weights = wa_ref[0, 0]
+        weights = wa_ref[0]
         g_attn = gres_ref[...].astype(BF)
         g_att = dot(g_attn, weights[:, 3 * local :]).astype(BF)
         g_att_t = g_att.T
@@ -496,9 +487,9 @@
 def backward_pass(tok, cot, vec, saved, wide, head):
     res, hm, h2, prob, keys, vals, query, att, act, slope = saved
     rows, width = tok.shape
-    groups = wide.shape[0]
+    groups = wide[0].shape[0]
     local = width // groups
-    hidden = wide.shape[3]
+    hidden = wide[1].shape[2]
     heads = local // head
     keyed = NB + rows
     first = lambda i: jnp.minimum(i, groups - 1)
@@ -521,14 +512,15 @@
             pl.BlockSpec((1, local, rows), lambda i: (second(i), 0, 0)),
             pl.BlockSpec((1, rows, hidden), lambda i: (first(i), 0, 0)),
             pl.BlockSpec((1, rows, hidden), lambda i: (first(i), 0, 0)),
-            pl.BlockSpec((1, 1, width, width), lambda i: (second(i), 0, 0, 0)),
-            pl.BlockSpec((1, 1, width, hidden), lambda i: (first(i), 1, 0, 0)),
-            pl.BlockSpec((1, 1, width, hidden), lambda i: (first(i), 2, 0, 0)),
+            pl.BlockSpec((1, width, width), lambda i: (second(i), 0, 0)),
+            pl.BlockSpec((1, width, hidden), lambda i: (first(i), 0, 0)),
+            pl.BlockSpec((1, width, hidden), lambda i: (first(i), 0, 0)),
         ],
         out_specs=[
             whole((rows, width)),
             whole((NB, width)),
-            pl.BlockSpec((1, 2, width, hidden), lambda i: (first(i), 0, 0, 0)),
+            pl.BlockSpec((1, width, hidden), lambda i: (first(i), 0, 0)),
+            pl.BlockSpec((1, width, hidden), lambda i: (first(i), 0, 0)),
             pl.BlockSpec((1, width, width), lambda i: (second(i), 0, 0)),
             whole((8, width)),
             pl.BlockSpec((1, 8, hidden), lambda i: (i, 0, 0)),
@@ -536,7 +528,8 @@
         out_shape=[
             jax.ShapeDtypeStruct((rows, width), BF),
             jax.ShapeDtypeStruct((NB, width), F32),
-            jax.ShapeDtypeStruct((groups, 2, width, hidden), BF),
+            jax.ShapeDtypeStruct((groups, width, hidden), BF),
+            jax.ShapeDtypeStruct((groups, width, hidden), BF),
             jax.ShapeDtypeStruct((groups, width, width), BF),
             jax.ShapeDtypeStruct((8, width), F32),
             jax.ShapeDtypeStruct((2 * groups, 8, hidden), F32),
@@ -552,8 +545,521 @@
         compiler_params=pltpu.CompilerParams(vmem_limit_bytes=BIG_VMEM),
         name="backward_pass",
     )(
-        tok, cot, res, vec, hm, h2, prob, keys, vals, query, att, act, slope, wide, wide, wide
+        tok, cot, res, vec, hm, h2, prob, keys, vals, query, att, act, slope, *wide
     )
+
+
+MESH = pl.DeviceIdType.MESH
+LINE = 4
+PLANE = 8
+NEAR = (0, -1, 1, -2, 2, -3, 3)
+FAR = (-3, 3, -2, 2, -1, 1, 0)
+
+
+class Place:
+    def __init__(self):
+        self.s = lax.axis_index("seq")
+        self.z = lax.axis_index("mp")
+        core = lax.rem(self.s, 2)
+        x = lax.rem(self.s // 2, 2)
+        y = self.s // 4
+        self.turn = 1 - 2 * core
+        self.partner = self.s + self.turn
+        self.sx = self.s + 2 - 4 * x
+        self.sy = self.s + 4 - 8 * y
+        self.sd = self.sx + 4 - 8 * y
+        self.low = self.z > 0
+        self.high = self.z < LINE - 1
+
+
+def valid(m):
+    return (m >= 0) & (m < LINE)
+
+
+def when(condition, act):
+    if condition is None:
+        act()
+    else:
+        pl.when(condition)(act)
+
+
+def greet(place, line=True, plane=True):
+    barrier = pltpu.get_barrier_semaphore()
+
+    def signal(seq, z):
+        pl.semaphore_signal(barrier, inc=1, device_id=(seq, z), device_id_type=MESH)
+
+    if plane:
+        for seq in (place.partner, place.sx, place.sy):
+            signal(seq, place.z)
+    if line:
+        pl.when(place.low)(lambda: signal(place.s, place.z - 1))
+        pl.when(place.high)(lambda: signal(place.s, place.z + 1))
+    peers = 3 if plane else 0
+    if line:
+        peers = peers + (place.z + LINE - 1) // LINE + (2 * LINE - 2 - place.z) // LINE
+    pl.semaphore_wait(barrier, peers)
+
+
+UP, DOWN, ACROSS_X, ACROSS_Y, PARTNER = range(5)
+
+
+class Spread:
+    def __init__(self, place, src, dst, send, recv, local, line=True):
+        self.p, self.src, self.dst = place, src, dst
+        self.send, self.recv, self.line = send, recv, line
+        self.rows = src.shape[0]
+        self.sent = []
+        self.own = pltpu.make_async_copy(src, self.at(self.mine(), place.s), local)
+
+    def mine(self):
+        return self.p.z if self.line else 0
+
+    def at(self, m, s):
+        return self.dst.at[m, pl.ds(s * self.rows, self.rows), :]
+
+    def copy(self, direction, m, s, own=False):
+        p = self.p
+        device = (
+            (p.s, p.z + 1),
+            (p.s, p.z - 1),
+            (p.sx, p.z),
+            (p.sy, p.z),
+            (p.partner, p.z),
+        )[direction]
+        return pltpu.make_async_remote_copy(
+            src_ref=self.src if own else self.at(m, s),
+            dst_ref=self.at(m, s),
+            send_sem=self.send.at[direction, m * 4 + s // 2],
+            recv_sem=self.recv.at[m * PLANE + s],
+            device_id=device,
+            device_id_type=MESH,
+        )
+
+    def start(self, condition, *what, **how):
+        when(condition, lambda: self.copy(*what, **how).start())
+        self.sent.append((condition, what, how))
+
+    def arrived(self, m, s):
+        self.copy(PARTNER, m, s).wait_recv()
+
+    def around(self):
+        if not self.line:
+            return [(0, None, 0)]
+        return [(d, valid(self.p.z + d), self.p.z + d) for d in NEAR]
+
+    def first(self):
+        p, m = self.p, self.mine()
+        self.own.start()
+        if self.line:
+            self.start(p.high, UP, m, p.s, own=True)
+            self.start(p.low, DOWN, m, p.s, own=True)
+        for direction in (ACROSS_X, ACROSS_Y, PARTNER):
+            self.start(None, direction, m, p.s, own=True)
+
+    def along(self):
+        p = self.p
+        for d, ok, m in self.around()[1:]:
+            when(ok, lambda: self.arrived(m, p.s))
+            if d < 0:
+                self.start(ok & p.high, UP, m, p.s)
+            else:
+                self.start(ok & p.low, DOWN, m, p.s)
+            for direction in (ACROSS_X, ACROSS_Y, PARTNER):
+                self.start(ok, direction, m, p.s)
+
+    def across(self):
+        p = self.p
+        for d, ok, m in self.around():
+            odd = lax.rem(m, 2) == 1 if self.line else None
+            when(ok, lambda: self.arrived(m, p.sx))
+            if self.line:
+                self.start(ok & odd, ACROSS_Y, m, p.sx)
+            self.start(ok, PARTNER, m, p.sx)
+            when(ok, lambda: self.arrived(m, p.sy))
+            self.start(ok & ~odd if self.line else None, ACROSS_X, m, p.sy)
+            self.start(ok, PARTNER, m, p.sy)
+
+    def corner(self):
+        p = self.p
+        for d, ok, m in self.around():
+            when(ok, lambda: self.arrived(m, p.sd))
+            self.start(ok, PARTNER, m, p.sd)
+
+    def finish(self):
+        p = self.p
+
+        @pl.loop(0, LINE if self.line else 1)
+        def _(m):
+            for s in (p.s, p.sx, p.sy, p.sd):
+                self.arrived(m, s + p.turn)
+
+        for condition, what, how in self.sent:
+            when(condition, lambda: self.copy(*what, **how).wait_send())
+        self.own.wait()
+
+
+def spread_kernel(*refs, count, line):
+    place = Place()
+    srcs, dsts = refs[:count], refs[count : 2 * count]
+    send, recv, local = refs[2 * count :]
+    greet(place, line)
+    parts = [
+        Spread(place, srcs[i], dsts[i], send.at[i], recv.at[i], local.at[i], line)
+        for i in range(count)
+    ]
+    for turn in range(count + 3):
+        for i in range(count):
+            stage = turn - i
+            if stage == 0:
+                parts[i].first()
+            elif stage == 1:
+                parts[i].along()
+            elif stage == 2:
+                parts[i].across()
+            elif stage == 3:
+                parts[i].corner()
+    for part in parts:
+        part.finish()
+
+
+def spread(blocks, collective_id, name, line=True):
+    count = len(blocks)
+    depth = LINE if line else 1
+    dma = pltpu.SemaphoreType.DMA
+    return pl.pallas_call(
+        functools.partial(spread_kernel, count=count, line=line),
+        out_shape=[
+            jax.ShapeDtypeStruct((depth, b.shape[0] * PLANE, b.shape[1]), b.dtype) for b in blocks
+        ],
+        in_specs=[pl.BlockSpec(memory_space=pl.ANY)] * count,
+        out_specs=[pl.BlockSpec(memory_space=pl.ANY)] * count,
+        scratch_shapes=[
+            dma((count, 5, depth * 4)),
+            dma((count, depth * PLANE)),
+            dma((count,)),
+        ],
+        compiler_params=pltpu.CompilerParams(collective_id=collective_id, has_side_effects=True),
+        name=name,
+    )(*blocks)
+
+
+class Line:
+    def __init__(self, place, src, dst, send, recv, local):
+        self.p, self.src, self.dst = place, src, dst
+        self.send, self.recv = send, recv
+        self.sent = []
+        self.own = pltpu.make_async_copy(src, dst.at[place.z], local)
+
+    def copy(self, up, m, own=False):
+        p = self.p
+        return pltpu.make_async_remote_copy(
+            src_ref=self.src if own else self.dst.at[m],
+            dst_ref=self.dst.at[m],
+            send_sem=self.send.at[1 if up else 0, m],
+            recv_sem=self.recv.at[m],
+            device_id=(p.s, p.z + 1 if up else p.z - 1),
+            device_id_type=MESH,
+        )
+
+    def start(self, condition, *what, **how):
+        when(condition, lambda: self.copy(*what, **how).start())
+        self.sent.append((condition, what, how))
+
+    def first(self):
+        p = self.p
+        self.own.start()
+        self.start(p.high, True, p.z, own=True)
+        self.start(p.low, False, p.z, own=True)
+
+    def step(self, distance):
+        p = self.p
+        for d in (-distance, distance):
+            m = p.z + d
+            ok = valid(m)
+            when(ok, lambda: self.copy(True, m).wait_recv())
+            if d < 0:
+                self.start(ok & p.high, True, m)
+            else:
+                self.start(ok & p.low, False, m)
+
+    def finish(self):
+        for condition, what, how in self.sent:
+            when(condition, lambda: self.copy(*what, **how).wait_send())
+        self.own.wait()
+
+
+def line_kernel(src, dst, send, recv, local):
+    place = Place()
+    greet(place, plane=False)
+    line = Line(place, src, dst, send, recv, local)
+    line.first()
+    for distance in range(1, LINE):
+        line.step(distance)
+    line.finish()
+
+
+def line_gather(block, collective_id, name):
+    dma = pltpu.SemaphoreType.DMA
+    return pl.pallas_call(
+        line_kernel,
+        out_shape=jax.ShapeDtypeStruct((LINE,) + block.shape, block.dtype),
+        in_specs=[pl.BlockSpec(memory_space=pl.ANY)],
+        out_specs=pl.BlockSpec(memory_space=pl.ANY),
+        scratch_shapes=[dma((2, LINE)), dma((LINE,)), dma(())],
+        compiler_params=pltpu.CompilerParams(collective_id=collective_id, has_side_effects=True),
+        name=name,
+    )(block)
+
+
+class Collect:
+    OWN, SIDE_X, SIDE_Y, CORNER = range(4)
+
+    def __init__(self, place, grads, out, buffers, sems):
+        self.p, self.grads, self.out = place, grads, out
+        self.mine, self.pin, self.din, self.xin, self.yin, self.uin, self.win = buffers
+        self.block_sems, self.sems = sems
+        self.rows = out.shape[0]
+        self.columns = (place.s, place.sx, place.sy, place.sd)
+
+    def unit(self, c, m, turn=0):
+        s = self.columns[c] + turn
+        return self.grads.at[m, pl.ds(s * self.rows, self.rows), :]
+
+    def load(self, c, m):
+        return pltpu.make_async_copy(
+            self.unit(c, m), self.mine.at[c, m], self.block_sems.at[0, c, m]
+        )
+
+    def remote(self, src, dst, send, recv, device):
+        return pltpu.make_async_remote_copy(
+            src_ref=src,
+            dst_ref=dst,
+            send_sem=send,
+            recv_sem=recv,
+            device_id=device,
+            device_id_type=MESH,
+        )
+
+    def swap(self, c, m):
+        p = self.p
+        return self.remote(
+            self.unit(c, m, p.turn),
+            self.pin.at[c, m],
+            self.block_sems.at[1, c, m],
+            self.block_sems.at[2, c, m],
+            (p.partner, p.z),
+        )
+
+    def hop(self, kind, m, by_x=True):
+        p = self.p
+        src, dst, device = (
+            (self.CORNER, self.din, (p.sx if by_x else p.sy, p.z)),
+            (self.SIDE_X, self.xin, (p.sx, p.z)),
+            (self.SIDE_Y, self.yin, (p.sy, p.z)),
+        )[kind]
+        return self.remote(
+            self.mine.at[src, m],
+            dst.at[m],
+            self.sems.at[kind, m],
+            self.sems.at[4 + kind, m],
+            device,
+        )
+
+    def climb(self, m, up):
+        p = self.p
+        return self.remote(
+            self.mine.at[self.OWN, m],
+            (self.uin if up else self.win).at[m],
+            self.sems.at[3, m],
+            self.sems.at[7 if up else 8, m],
+            (p.s, p.z + 1 if up else p.z - 1),
+        )
+
+    def add(self, c, m, *others):
+        total = self.mine[c, m].astype(F32)
+        for other in others:
+            total = total + other[m].astype(F32)
+        self.mine[c, m] = total.astype(BF)
+
+    def ring(self, body):
+        for d in FAR:
+            m = self.p.z + d
+            pl.when(valid(m))(functools.partial(body, d, m))
+
+    def begin(self):
+        for c in (self.CORNER, self.SIDE_X, self.SIDE_Y, self.OWN):
+
+            @pl.loop(0, LINE)
+            def _(m):
+                self.load(c, m).start()
+                self.swap(c, m).start()
+
+    def join(self, c, m):
+        self.load(c, m).wait()
+        self.swap(c, m).wait_recv()
+        self.add(c, m, self.pin.at[c])
+
+    def corner(self):
+        def body(d, m):
+            self.join(self.CORNER, m)
+            even = lax.rem(m, 2) == 0
+            pl.when(even)(lambda: self.hop(0, m, True).start())
+            pl.when(~even)(lambda: self.hop(0, m, False).start())
+
+        self.ring(body)
+
+    def sides(self):
+        def body(d, m):
+            even = lax.rem(m, 2) == 0
+            self.join(self.SIDE_X, m)
+            self.join(self.SIDE_Y, m)
+            pl.when(even)(lambda: self.hop(1, m).start())
+            pl.when(~even)(lambda: self.hop(2, m).start())
+
+        self.ring(body)
+
+    def relay(self):
+        def body(d, m):
+            even = lax.rem(m, 2) == 0
+            self.hop(0, m).wait_recv()
+
+            @pl.when(even)
+            def _():
+                self.add(self.SIDE_Y, m, self.din)
+                self.hop(2, m).start()
+
+            @pl.when(~even)
+            def _():
+                self.add(self.SIDE_X, m, self.din)
+                self.hop(1, m).start()
+
+        self.ring(body)
+
+    def line(self):
+        p = self.p
+
+        def body(d, m):
+            self.join(self.OWN, m)
+            self.hop(1, m).wait_recv()
+            self.hop(2, m).wait_recv()
+            self.add(self.OWN, m, self.xin, self.yin)
+            if d > 0:
+
+                @pl.when(p.low)
+                def _():
+                    self.climb(m, True).wait_recv()
+                    self.add(self.OWN, m, self.uin)
+
+                self.climb(m, True).start()
+            elif d < 0:
+
+                @pl.when(p.high)
+                def _():
+                    self.climb(m, False).wait_recv()
+                    self.add(self.OWN, m, self.win)
+
+                self.climb(m, False).start()
+
+        self.ring(body)
+
+    def result(self):
+        p = self.p
+        self.out[...] = self.mine[self.OWN, p.z].astype(F32)
+
+        @pl.when(p.low)
+        def _():
+            self.climb(p.z, True).wait_recv()
+            self.out[...] += self.uin[p.z].astype(F32)
+
+        @pl.when(p.high)
+        def _():
+            self.climb(p.z, False).wait_recv()
+            self.out[...] += self.win[p.z].astype(F32)
+
+    def finish(self):
+        for c in range(4):
+
+            @pl.loop(0, LINE)
+            def _(m):
+                self.swap(c, m).wait_send()
+
+        @pl.loop(0, LINE)
+        def _(m):
+            for kind in range(3):
+                self.hop(kind, m).wait_send()
+            pl.when(m != self.p.z)(lambda: self.climb(m, True).wait_send())
+
+
+BUFFERS = ((4, LINE), (4, LINE), (LINE,), (LINE,), (LINE,), (LINE,), (LINE,))
+
+
+def collect_kernel(*refs, count):
+    place = Place()
+    grads, rows = refs[:count], refs[count]
+    outs, all_rows = refs[count + 1 : 2 * count + 1], refs[2 * count + 1]
+    rest = refs[2 * count + 2 :]
+    buffers, (block_sems, sems, line_send, line_recv, line_own) = rest[:-5], rest[-5:]
+    greet(place)
+    parts = [
+        Collect(
+            place, grads[i], outs[i], buffers[i :: count], (block_sems.at[i], sems.at[i])
+        )
+        for i in range(count)
+    ]
+    line = Line(place, rows, all_rows, line_send, line_recv, line_own)
+    for part in parts:
+        part.begin()
+    for turn in range(count + 4):
+        if turn == 1:
+            line.first()
+        elif turn == 2:
+            line.step(1)
+        elif turn == 4:
+            line.step(2)
+        elif turn == 5:
+            line.step(3)
+        for i in range(count):
+            stage = turn - i
+            if stage == 0:
+                parts[i].corner()
+            elif stage == 1:
+                parts[i].sides()
+            elif stage == 2:
+                parts[i].relay()
+            elif stage == 3:
+                parts[i].line()
+            elif stage == 4:
+                parts[i].result()
+    for part in parts:
+        part.finish()
+    line.finish()
+
+
+def collect(grads, rows, collective_id):
+    count = len(grads)
+    dma = pltpu.SemaphoreType.DMA
+    anywhere = pl.BlockSpec(memory_space=pl.ANY)
+    blocks = [(g.shape[1] // PLANE, g.shape[2]) for g in grads]
+    return pl.pallas_call(
+        functools.partial(collect_kernel, count=count),
+        out_shape=[jax.ShapeDtypeStruct(b, F32) for b in blocks]
+        + [jax.ShapeDtypeStruct((LINE,) + rows.shape, rows.dtype)],
+        in_specs=[anywhere] * (count + 1),
+        out_specs=[pl.BlockSpec(memory_space=pltpu.VMEM)] * count + [anywhere],
+        scratch_shapes=[pltpu.VMEM(lead + b, BF) for lead in BUFFERS for b in blocks]
+        + [
+            dma((count, 3, 4, LINE)),
+            dma((count, 9, LINE)),
+            dma((2, LINE)),
+            dma((LINE,)),
+            dma(()),
+        ],
+        compiler_params=pltpu.CompilerParams(
+            collective_id=collective_id, has_side_effects=True, vmem_limit_bytes=BIG_VMEM
+        ),
+        name="collect_grads",
+    )(*grads, rows)
 
 
 def local(
@@ -576,43 +1082,60 @@
     b_down,
 ):
     seq, mp = lax.axis_size("seq"), lax.axis_size("mp")
-    mp_index = lax.axis_index("mp")
-    both = ("seq", "mp")
+    seq_index, mp_index = lax.axis_index("seq"), lax.axis_index("mp")
     item_count, seg_len, local_width = past_state.shape
     slots = positions.shape[1]
     total = item_count * seq
     width = tokens.shape[1]
     part = width // seq
-    heads_local = b_qv.shape[1]
-    piece = b_qv.shape[2]
+    heads_local, piece = b_qv.shape[1], b_qv.shape[2]
     head = piece * seq
     hidden = w_up.shape[1]
     rows = tokens.shape[0] // mp
-
+    direct = seq == PLANE and mp == LINE and part % 16 == 0 and hidden == width
+    mem_rows = NB // (seq * mp)
+
+    items = (seq_index * item_count + jnp.arange(item_count)).astype(F32)
+    places = (items[:, None] + (positions.astype(F32) + 0.5) / seg_len) / total
+    used = (jnp.arange(slots)[None, :] < counts[:, None]).astype(F32)
+    meta = jnp.concatenate([places, used, jnp.zeros((8 - 2 * item_count, slots), F32)])
     pos3 = positions.reshape(item_count, slots, 1)
-    counts3 = counts.reshape(item_count, 1, 1)
-    sampled = sample_rows(past_state, pos3)
-    all_sampled = lax.all_gather(sampled, "seq", axis=0, tiled=True)
-    all_pos = lax.all_gather(positions, "seq", axis=0, tiled=True).reshape(total, slots, 1)
-    all_counts = lax.all_gather(counts, "seq", axis=0, tiled=True).reshape(total, 1, 1)
-    coef_part, inverse = solve_memory(all_sampled, all_pos, all_counts, seg_len)
-    coef = lax.all_gather(coef_part, "mp", axis=1, tiled=True)
-
-    shard = jnp.stack(
-        [jnp.concatenate([w_qkv[0], w_qkv[1], w_qkv[2], w_out.T], axis=1), w_up, w_down.T]
-    )
-    wide = lax.all_gather(lax.all_gather(shard, "seq", axis=1, tiled=True), "mp", axis=0)
+    sampled = sample_rows(past_state, pos3).reshape(item_count * slots, local_width)
+    if direct:
+        all_sampled, all_meta = spread([sampled, meta], 1, "spread_samples", line=False)
+    else:
+        all_sampled = lax.all_gather(sampled, "seq", axis=0)
+        all_meta = lax.all_gather(meta, "seq", axis=0)
+    all_sampled = all_sampled.reshape(seq, item_count * slots, local_width)
+    coef_part, inverse = solve_memory(all_sampled, all_meta.reshape(seq, 8, slots), item_count)
+    if direct:
+        coef = line_gather(coef_part, 2, "line_coef")
+    else:
+        coef = lax.all_gather(coef_part, "mp", axis=0)
+    coef = coef.transpose(1, 0, 2).reshape(NB, width)
+
+    attn = jnp.concatenate([w_qkv[0], w_qkv[1], w_qkv[2], w_out.T], axis=1)
     small = jnp.concatenate(
         [ln1_gain, ln1_bias, ln2_gain, ln2_bias, b_out, b_down, b_qv.reshape(-1), b_up.reshape(-1)]
     )
-    small = lax.all_gather(lax.all_gather(small, "seq", axis=0), "mp", axis=0)
+    if direct:
+        room = jnp.zeros((16, width), BF).at[0, : small.shape[0]].set(small)
+        room, *wide = spread([room, attn, w_up, w_down.T], 3, "spread_weights")
+        small = room.reshape(mp, seq, 16, width)[:, :, 0]
+    else:
+        wide = [
+            lax.all_gather(lax.all_gather(shard, "seq", axis=0, tiled=True), "mp", axis=0)
+            for shard in (attn, w_up, w_down.T)
+        ]
+        small = lax.all_gather(lax.all_gather(small, "seq", axis=0), "mp", axis=0)
     vec = small[0, :, : 6 * part].reshape(seq, 6, part).transpose(1, 0, 2).reshape(6, width)
     vec = jnp.concatenate([vec, jnp.zeros((2, width), BF)]).astype(F32)
     at = 6 * part
     size = 2 * heads_local * piece
+    up_size = hidden // seq
     bias_qv = small[:, :, at : at + size].reshape(mp, seq, 2, heads_local, piece)
     bias_qv = bias_qv.transpose(0, 2, 3, 1, 4).reshape(mp, 2, local_width)
-    bias_up = small[:, :, at + size :].reshape(mp, seq, -1, piece)
+    bias_up = small[:, :, at + size : at + size + up_size].reshape(mp, seq, -1, piece)
     bias_up = bias_up.transpose(0, 2, 1, 3).reshape(mp, hidden)
     zero = jnp.zeros((mp, local_width), BF)
     first = jnp.concatenate([bias_qv[:, 0], zero, bias_qv[:, 1], zero], axis=1)
@@ -624,44 +1147,61 @@
     cot = lax.dynamic_slice_in_dim(cotangent, mp_index * rows, rows, 0)
     forward = forward_pass(tok, coef, vec, gvec, wide, head)
     block_out = lax.all_gather(forward[0], "mp", axis=0, tiled=True)
-    tok_grad, gmem, g_mlp, g_att, gv, ggv = backward_pass(tok, cot, vec, forward[1:], wide, head)
-    block_grad = lax.all_gather(tok_grad, "mp", axis=0, tiled=True)
-
-    gmem, gv, ggv = lax.psum((gmem, gv, ggv), both)
-    past_grad, gv_mem = past_grads(
-        gmem, coef, vec, inverse, pos3, counts3, total, seg_len, local_width
+    tok_grad, gmem, g_up, g_down, g_attn, gv, ggv = backward_pass(
+        tok, cot, vec, forward[1:], wide, head
     )
-    gv = gv + gv_mem
-
-    grads = jnp.concatenate([g_att[:, None], g_mlp], axis=1)
-    grads = lax.psum_scatter(grads, "mp", scatter_dimension=0, tiled=False)
-    grads = lax.psum_scatter(grads, "seq", scatter_dimension=1, tiled=True).astype(F32)
-    attn = grads[0]
+
+    tail = gv[:6].reshape(6, seq, part).transpose(1, 0, 2).reshape(1, seq, 6 * part)
+    tail = jnp.broadcast_to(tail, (mp, seq, 6 * part))
+    qv = ggv[mp:, 0]
+    qv = jnp.stack([qv[:, :local_width], qv[:, 2 * local_width : 3 * local_width]], axis=1)
+    qv = qv.reshape(mp, 2, heads_local, seq, piece).transpose(0, 3, 1, 2, 4).reshape(mp, seq, size)
+    up = ggv[:mp, 0].reshape(mp, -1, seq, piece).transpose(0, 2, 1, 3).reshape(mp, seq, up_size)
+    tail = jnp.concatenate([tail, qv, up], axis=2)
+    if direct:
+        tail = jnp.pad(tail, ((0, 0), (0, 0), (0, width - tail.shape[2])))[:, :, None]
+        mem = gmem.reshape(mp, seq, mem_rows, width)
+        pad = jnp.zeros((mp, seq, 15 - mem_rows, width), F32)
+        side = jnp.concatenate([mem, tail, pad], axis=2).astype(BF).reshape(mp, seq * 16, width)
+        side, attn, up_grad, down_grad, block_grad = collect(
+            [side, g_attn, g_up, g_down], tok_grad, 4
+        )
+        block_grad = block_grad.reshape(mp * rows, width)
+        (gmem,) = spread([side[:mem_rows]], 5, "spread_memory")
+        gmem = gmem.reshape(NB, width)
+        own = side[mem_rows]
+    else:
+        block_grad = lax.all_gather(tok_grad, "mp", axis=0, tiled=True)
+        gmem, tail = lax.psum((gmem, tail), ("seq", "mp"))
+        own = tail[mp_index, seq_index]
+        attn, up_grad, down_grad = (
+            lax.psum_scatter(
+                lax.psum_scatter(g, "mp", scatter_dimension=0, tiled=False),
+                "seq",
+                scatter_dimension=0,
+                tiled=True,
+            ).astype(F32)
+            for g in (g_attn, g_up, g_down)
+        )
+    past_grad, gv_mem = past_grads(gmem, coef, vec, inverse, meta, pos3, seg_len, local_width)
+    gv_own = lax.dynamic_slice_in_dim(gv_mem, seq_index * part, part, 1)
+    vec_own = own[: 6 * part].reshape(6, part)
     qkv_grad = jnp.stack([attn[:, i * local_width : (i + 1) * local_width] for i in range(3)])
-    out_grad = attn[:, 3 * local_width :].T
-    seq_index = lax.axis_index("seq")
-    vec_own = lax.dynamic_slice_in_dim(gv, seq_index * part, part, 1)
-    qv = lax.dynamic_slice_in_dim(ggv, mp + mp_index, 1, 0)[0, 0]
-    qv = jnp.stack([qv[:local_width], qv[2 * local_width : 3 * local_width]])
-    qv = qv.reshape(2, heads_local, head)
-    qv = lax.dynamic_slice_in_dim(qv, seq_index * piece, piece, 2)
-    up = lax.dynamic_slice_in_dim(ggv, mp_index, 1, 0)[0, 0].reshape(-1, head)
-    up = lax.dynamic_slice_in_dim(up, seq_index * piece, piece, 1)
     return (
         block_out,
         block_grad,
         past_grad,
-        vec_own[0],
-        vec_own[1],
+        vec_own[0] + gv_own[0],
+        vec_own[1] + gv_own[1],
         qkv_grad,
-        qv,
-        out_grad,
+        own[at : at + size].reshape(2, heads_local, piece),
+        attn[:, 3 * local_width :].T,
         vec_own[4],
         vec_own[2],
         vec_own[3],
-        grads[1],
-        up,
-        grads[2].T,
+        up_grad,
+        own[at + size : at + size + up_size].reshape(-1, piece),
+        down_grad.T,
         vec_own[5],
     )
 

time: 960 us -> 424 us (0.44)
  waiting for transfers between devices: 621 us -> 0.02 us
  Pallas kernels: 126 us -> 357 us
  blocking collectives: 144 us -> 0 us
  other arithmetic: 18.7 us -> 8.84 us
    reduce_scatter x2 -> x0, waiting for transfers between devices: 284 us -> none  [the longest x1 234 us: local(): grads = lax.psum_scatter(grads, 'mp', scatter_dimension=0, tiled=False)]
    pallas_call x2 -> x7, Pallas kernels: 45.3 us -> 277 us  [the longest x3 115 us: spread(): pl.pallas_call(functools.partial(spread_kernel, count=count, line=line),...]
    all_gather x3 -> x0, waiting for transfers between devices: 177 us -> none  [the longest x1 88.9 us: local(): lax.all_gather(lax.all_gather(shard, 'seq', axis=1, tiled=True), 'mp', ax...]
    psum x1 -> x0, waiting for transfers between devices: 93.3 us -> none  [local(): gmem, gv, ggv = lax.psum((gmem, gv, ggv), both)]
    all_gather x4 -> x0, blocking collectives: 71.6 us -> none  [the longest x1 29.1 us: local(): coef = lax.all_gather(coef_part, 'mp', axis=1, tiled=True)]
    all_gather x1, waiting for transfers between devices: 63.7 us -> 0.01 us  [local(): block_out = lax.all_gather(forward[0], 'mp', axis=0, tiled=True)]
    psum x1 -> x0, blocking collectives: 41.9 us -> none  [local(): gmem, gv, ggv = lax.psum((gmem, gv, ggv), both)]
    unnamed x2 -> x0, blocking collectives: 30.7 us -> none
  transfers between devices with their start and end apart: 7 -> 1, of which waited for: 7 -> 0; matrix products, arithmetic and copies ran while one was open for 3% -> 4% of each run, Pallas kernels for 5% -> 42%
where the time goes in v2:
time: 424 us; the launch traced here: 417 us
  Pallas kernels  357 us (84%)
  local copies, waits for them, and re-layouts  35.9 us (8%)
  between operations  14.8 us (3%)
  other arithmetic  8.84 us (2%)
    pallas_call x3, Pallas kernels, spread(): pl.pallas_call(functools.partial(spread_kernel, count=count, line=line),...  115 us
    pallas_call x1, Pallas kernels, collect(): pl.pallas_call(functools.partial(collect_kernel, count=count), out_shape=...  103 us
    pallas_call x1, Pallas kernels, backward_pass(): pl.pallas_call(functools.partial(backward_kernel, groups=groups, head=hea...  44.3 us
    pallas_call x1, Pallas kernels, solve_memory(): pl.pallas_call(functools.partial(solve_kernel, items=items), out_shape=(j...  36.8 us
    pallas_call x1, Pallas kernels, forward_pass(): pl.pallas_call(functools.partial(forward_kernel, groups=groups, head=head...  34.4 us
    unnamed x23, local copies, waits for them, and re-layouts  15.8 us
    pallas_call x1, Pallas kernels, line_gather(): pl.pallas_call(line_kernel, out_shape=jax.ShapeDtypeStruct((LINE,) + bloc...  15 us
  transfers between devices with their start and end apart: 1, of which 0 were waited for; matrix products, arithmetic and copies ran while one was open for 4% of the time, Pallas kernels for 42%

profile of v2, /device:TPU:0, one launch (start us, length us, event | category | flops | bytes accessed | tf_op | source)
XLA Modules:
  0.0 416.9 jit_solution(11554941771042698865)
XLA Ops:
  7.2 0.9 slice_bitcast_fusion.6
  8.1 0.9 copy.120
  9.0 0.8 copy.119
  9.7 0.1 reshape.168
  9.8 0.7 copy.118
  10.5 0.1 reshape.167
  10.6 4.1 concatenate.31
  14.7 0.6 scatter.4.refs_0_
  15.3 0.8 pad_maximum_fusion.1.refs_1_
  16.1 80.1 %spread_weights.1 = (bf16[4,128,768]{2,1,0:T(8,128)(2,1)}, bf16[4,768,768]{2,1,0:T(8,128)(2,1)}, bf16[4,768,768]{2,1,0:T(8,128)(2,1)}, bf16[4,768,768]{2,1,0:T(8,128)(2,1)}) custom-call(bf16[16,768]{1,0:T(8,128)(2,1)} %scatter.4.refs_0_, bf16[96,768]{1,0:T(8,128)(2,1)} %pad_maximum_fusion.1.refs_1_, bf16[96,768]{1,0:T(8,128)(2,1)} %refs_2_.1, ...), custom_call_target="tpu_custom_call" | custom-call | tf_op jit(solution)/shard_map/spread_weights/pallas_call | solution.py:730
  96.2 1.1 slice.155
  97.4 0.1 reshape.172
  97.5 0.1 reshape.173
  97.8 0.2 reshape.174
  98.0 0.1 broadcast_in_dim_reshape.4
  98.1 0.1 reshape_squeeze.7
  98.2 0.1 reshape.171
  98.3 0.6 pad_convert_fusion.vec_ref
  98.9 0.7 compare_convert_fusion
  99.6 0.7 add_multiply_fusion
  100.4 1.5 copy.116.pos_ref
  101.9 2.0 copy.115.past_ref
  103.9 2.1 sample_rows.1
  106.0 0.7 maximum_maximum_fusion.1.refs_1_.meta_ref
  106.7 15.5 %spread_samples.1 = (bf16[1,2048,192]{2,1,0:T(8,128)(2,1)}, f32[1,64,128]{2,1,0:T(8,128)}) custom-call(bf16[256,192]{1,0:T(8,128)(2,1)} %bitcast.75, f32[8,128]{1,0:T(8,128)} %maximum_maximum_fusion.1.refs_1_.meta_ref), custom_call_target="tpu_custom_call" | custom-call | tf_op jit(solution)/shard_map/spread_samples/pallas_call | solution.py:730
  122.2 36.8 %solve_memory.1 = (bf16[256,192]{1,0:T(8,128)(2,1)}, f32[256,256]{1,0:T(8,128)}) custom-call(bf16[8,256,192]{2,1,0:T(8,128)(2,1)} %bitcast.73, f32[8,8,128]{2,1,0:T(8,128)} %bitcast.86), custom_call_target="tpu_custom_call" | custom-call | tf_op jit(solution)/shard_map/solve_memory/pallas_call | solution.py:149
  159.0 15.0 %line_coef.1 = bf16[4,256,192]{2,1,0:T(8,128)(2,1)} custom-call(bf16[256,192]{1,0:T(8,128)(2,1)} %get-tuple-element.62.src), custom_call_target="tpu_custom_call" | custom-call | tf_op jit(solution)/shard_map/line_coef/pallas_call | solution.py:804
  174.0 1.2 copy.117
  175.2 1.0 copy.127.coef_ref
  176.3 0.7 maximum_convert_fusion.gvec_ref
  177.0 2.6 constant_dynamic-slice_fusion.1
  179.6 34.4 %forward_pass.1 = (bf16[512,768]{1,0:T(8,128)(2,1)}, f32[512,768]{1,0:T(8,128)}, bf16[768,768]{1,0:T(8,128)(2,1)}, bf16[512,768]{1,0:T(8,128)(2,1)}, bf16[4,3,76...) custom-call(bf16[512,768]{1,0:T(8,128)(2,1)} %get-tuple-element.191., ...), custom_call_target="tpu_custom_call" | custom-call | tf_op jit(solution)/shard_map/forward_pass/pallas_call | solution.py:304
  214.1 44.3 %backward_pass.1 = (bf16[512,768]{1,0:T(8,128)(2,1)}, f32[256,768]{1,0:T(8,128)}, bf16[4,768,768]{2,1,0:T(8,128)(2,1)}, bf16[4,768,768]{2,1,0:T(8,128)(2,1)}, bf...) custom-call(bf16[512,768]{1,0:T(8,128)(2,1)} %get-tuple-element.191.tok_ref, ...), custom_call_target="tpu_custom_call" | custom-call | tf_op jit(solution)/shard_map/backward_pass/pallas_call | solution.py:498
  258.4 1.0 fusion.7
  259.4 0.1 stack.21
  259.5 0.1 stack.22
  259.7 0.1 reshape.177
  259.8 0.1 reshape_squeeze.8
  260.0 0.1 reshape.178
  260.1 0.7 slice.186
  260.9 0.1 reshape.185
  261.0 0.1 reshape.183
  261.1 0.1 fusion.5
  261.2 1.2 convert.32
  262.5 1.1 maximum_maximum_fusion
  263.6 103.0 %collect_grads.1 = (f32[16,768]{1,0:T(8,128)}, f32[96,768]{1,0:T(8,128)}, f32[96,768]{1,0:T(8,128)}, f32[96,768]{1,0:T(8,128)}, bf16[4,512,768]{2,1,0:T(8,128)(2,1)}) custom-call(bf16[4,128,768]{2,1,0:T(8,128)(2,1)} %bitcast.69, bf16[4,768,768]{2,1,0:T(8,128)(2,1)} %get-tuple-element.81.refs_1_, bf16[4,768,768]{2,1,0:T(8,128)(2,1)} %get-tuple-element.82.refs_2_, ...), custom_call_target="tpu_custom_call" | custom-call | tf_op jit(solution)/shard_map/collect_grads/pallas_call | solution.py:1044
  366.7 1.4 slice.140.refs_0_
  368.1 19.6 %spread_memory.1 = f32[4,64,768]{2,1,0:T(8,128)} custom-call(f32[8,768]{1,0:T(8,128)} %slice.140.refs_0_), custom_call_target="tpu_custom_call" | custom-call | tf_op jit(solution)/shard_map/spread_memory/pallas_call | solution.py:730
  387.7 6.5 %past_grads.1 = (f32[2,512,192]{2,1,0:T(8,128)}, f32[8,768]{1,0:T(8,128)}) custom-call(f32[256,768]{1,0:T(8,128)} %bitcast.68, bf16[256,768]{1,0:T(8,128)(2,1)} %copy.127.coef_ref, f32[8,768]{1,0:T(8,128)} %pad_convert_fusion.vec_ref, f32[256,256]{1,0:T(8,128)} %get-tuple-element.87.inv_ref, f32[8,128]{1,0:T(8,128)} %maximum_maximum_fusion.1.refs_1_.meta_ref, ...), custom_call_target="tpu_custom_call" | custom-call | tf_op jit(solution)/shard_map/past_grads/pallas_call | solution.py:187
  394.2 0.8 constant_dynamic-slice_fusion
  394.9 1.4 slice_bitcast_fusion.7
  396.3 0.1 reshape.182
  396.4 0.7 copy.138
  397.1 2.4 copy.135
  399.5 0.1 slice_bitcast_fusion
  399.6 0.7 copy.137
  400.4 0.8 slice_reduce_fusion.1
  401.1 0.1 reshape.181
  401.2 0.6 copy.136
  401.8 0.7 pad_maximum_fusion
  402.5 3.9 copy.155
  406.5 1.7 copy.156
  408.1 0.7 copy.157
  408.8 0.7 copy.158
  (40 shorter events, 0.9 us)
Async XLA Ops:
  7.2 395.4 %all-gather.2.cloned.1.call-start = ((), (), s32[]{:S(2)}) async-start(), calls=%async_computation | async-start | bytes 3932160 | tf_op jit(solution)/shard_map/all_gather | solution.py:1149
  366.6 32.9 %copy-start.1 = (f32[96,768]{1,0:T(8,128)S(1)}, f32[96,768]{1,0:T(8,128)}, u32[]{:S(2)}) copy-start(f32[96,768]{1,0:T(8,128)} %get-tuple-element.90) | copy-start | bytes 884740
  402.5 3.9 copy-start
  406.5 1.7 copy-start.3
  406.5 2.4 copy-start.2
Sparse Core Ops, SparseCore 0:
  214.2 65.2 all-gather.1
